TPU v7x, 32 devices: a whole 2x2x4 slice. The times are simulated.
32 devices in a mesh: grp: 8 (over z, x), mem: 4 (over y, core).
Axes of the slice: x: 2, y: 2, z: 4, core: 2. Of those that a mesh axis runs over, the one named last changes fastest.
Arguments:
- tokens: bfloat16 [8, 4096, 1152], P('grp', 'mem'), may hold values from -6 to 6
- attn_gain: bfloat16 [1152], P('mem'), may hold values from 0.5 to 1.5
- mlp_gain: bfloat16 [1152], P('mem'), may hold values from 0.5 to 1.5
- query_weight: bfloat16 [1152, 1152], P('grp', 'mem'), may hold values from -0.1875 to 0.1875
- key_matrix: bfloat16 [1152, 384], P('grp', 'mem'), may hold values from -0.1875 to 0.1875
- value_matrix: bfloat16 [1152, 384], P('grp', 'mem'), may hold values from -0.1875 to 0.1875
- output_weight: bfloat16 [1152, 1152], P('grp', 'mem'), may hold values from -4 to 4
- gate_weight: bfloat16 [1152, 3072], P('grp', 'mem'), may hold values from -0.1875 to 0.1875
- up_weight: bfloat16 [1152, 3072], P('grp', 'mem'), may hold values from -0.1875 to 0.1875
- down_weight: bfloat16 [3072, 1152], P('grp', 'mem'), may hold values from -0.109375 to 0.109375
- cotangent: bfloat16 [8, 4096, 1152], P('grp', 'mem'), may hold values from -6 to 6
Outputs:
- output: bfloat16 [8, 4096, 1152], P('grp', 'mem')
- tokens_grad: bfloat16 [8, 4096, 1152], P('grp', 'mem')
- attn_gain_grad: float32 [1152], P('mem')
- mlp_gain_grad: float32 [1152], P('mem')
- query_weight_grad: float32 [1152, 1152], P('grp', 'mem')
- key_weight_grad: float32 [1152, 384], P('grp', 'mem')
- value_weight_grad: float32 [1152, 384], P('grp', 'mem')
- output_weight_grad: float32 [1152, 1152], P('grp', 'mem')
- gate_weight_grad: float32 [1152, 3072], P('grp', 'mem')
- up_weight_grad: float32 [1152, 3072], P('grp', 'mem')
- down_weight_grad: float32 [3072, 1152], P('grp', 'mem')
All inputs are finite; a program needn't handle non-finite values.
Results may differ from a plain program's by a relative error of at most 0.017.
Values may be sent and summed in bfloat16 or wider, within the bound.
No kernel may reach another device: no remote copies, remote signals or barrier semaphores. Data moves between devices by JAX's collectives and lax.ppermute only.
A program may use at most 384 MiB of HBM per device.

v0:
```python
import jax
import jax.numpy as jnp
from jax import lax
from jax.sharding import PartitionSpec as P

QUERY_HEADS = 18
KEY_VALUE_HEADS = 6
HEAD_SIZE = 64
CONT_LEN = 128
QUERY_BLOCK_ROWS = 512


EPSILON = 1e-05
NEG_FILL = -1e30


def broadcast(value, axis, source):
    kept = jnp.where(lax.axis_index(axis) == source, value, 0).astype(value.dtype)
    return lax.psum(kept, axis)


def matrix_product(left, right):
    return jnp.dot(left, right, preferred_element_type=jnp.float32)


def matmul_tn(left, right):
    return lax.dot_general(
        left, right, (((0,), (0,)), ((), ())), preferred_element_type=jnp.float32
    )


def matrix_product_transposed(left, right):
    return lax.dot_general(
        left, right, (((1,), (1,)), ((), ())), preferred_element_type=jnp.float32
    )


def assemble(piece, groups, members):
    height = piece.shape[1]
    width = piece.shape[2]
    return (
        piece.reshape(groups, members, height, width)
        .transpose(0, 2, 1, 3)
        .reshape(groups * height, members * width)
    )


def disperse(full, groups, members):
    height = full.shape[0] // groups
    width = full.shape[1] // members
    return (
        full.reshape(groups, height, members, width)
        .transpose(0, 2, 1, 3)
        .reshape(groups * members, height, width)
    )


def unpack(gathered, groups, members):
    gain_one = gathered[0].reshape(groups, members, -1)[0].reshape(-1)
    gain_two = gathered[1].reshape(groups, members, -1)[0].reshape(-1)
    matrices = tuple((assemble(piece, groups, members) for piece in gathered[2:]))
    return (gain_one, gain_two, matrices)


def tile_gain(gain_grad, groups, members):
    width = gain_grad.shape[0] // members
    return jnp.broadcast_to(gain_grad.reshape(1, members, width), (groups, members, width)).reshape(
        groups * members, width
    )


def rope_tables(token_positions):
    half = HEAD_SIZE // 2
    freq = 10000.0 ** (-jnp.arange(half, dtype=jnp.float32) * 2.0 / HEAD_SIZE)
    angle = token_positions.astype(jnp.float32)[:, None] * freq[None, :]
    return (jnp.cos(angle)[:, None, :], jnp.sin(angle)[:, None, :])


def rotary_apply(rows, cosine_table, sine_table, direction):
    half = rows.shape[-1] // 2
    first = rows[..., :half]
    second = rows[..., half:]
    return jnp.concatenate(
        [
            first * cosine_table - direction * second * sine_table,
            second * cosine_table + direction * first * sine_table,
        ],
        axis=-1,
    )


def norm_forward(rows, gain):
    inverse = lax.rsqrt(jnp.mean(rows * rows, axis=-1, keepdims=True) + EPSILON)
    return ((rows * inverse * gain.astype(jnp.float32)).astype(jnp.bfloat16), inverse)


def norm_backward(rows, inverse, gain, upstream):
    scaled = upstream * gain
    gain_grad = jnp.sum(upstream * rows * inverse, axis=0)
    inner = jnp.sum(scaled * rows, axis=-1, keepdims=True)
    rows_grad = scaled * inverse - rows * inverse**3 * inner / rows.shape[-1]
    return (rows_grad, gain_grad)


def prompt_forward(
    query_rows_list, key_rows_list, value_rows_list, prompt_key_rows, prompt_value_rows
):
    scale = HEAD_SIZE ** (-0.5)
    mixed_parts = []
    lse_parts = []
    for block in range(query_rows_list.shape[0] // QUERY_BLOCK_ROWS):
        start = block * QUERY_BLOCK_ROWS
        stop = start + QUERY_BLOCK_ROWS
        scores = (
            jnp.einsum(
                "rhgd,lhd->hgrl",
                query_rows_list[start:stop],
                key_rows_list[:stop],
                preferred_element_type=jnp.float32,
            )
            * scale
        )
        allowed = jnp.arange(stop)[None, :] <= (start + jnp.arange(QUERY_BLOCK_ROWS))[:, None]
        scores = jnp.where(allowed, scores, NEG_FILL)
        peak = jnp.max(scores, axis=-1, keepdims=True)
        raised = jnp.exp(scores - peak)
        total = jnp.sum(raised, axis=-1, keepdims=True)
        probs_low = (raised / total).astype(jnp.bfloat16)
        mixed_heads = jnp.einsum(
            "hgrl,lhd->rhgd", probs_low, value_rows_list[:stop], preferred_element_type=jnp.float32
        )
        mixed_parts.append(mixed_heads.astype(jnp.bfloat16).reshape(QUERY_BLOCK_ROWS, -1))
        lse_parts.append(peak + jnp.log(total))
    return (jnp.concatenate(mixed_parts, axis=0), jnp.stack(lse_parts))


def continuation_forward(
    query_rows_list, key_rows_list, value_rows_list, prompt_key_rows, prompt_value_rows
):
    heads_kv, head_group, depth = (
        query_rows_list.shape[1],
        query_rows_list.shape[2],
        query_rows_list.shape[3],
    )
    scale = HEAD_SIZE ** (-0.5)
    segments = QUERY_BLOCK_ROWS // CONT_LEN
    causal = jnp.arange(CONT_LEN)[None, :] <= jnp.arange(CONT_LEN)[:, None]
    mixed_parts = []
    lse_parts = []
    for block in range(query_rows_list.shape[0] // QUERY_BLOCK_ROWS):
        start = block * QUERY_BLOCK_ROWS
        stop = start + QUERY_BLOCK_ROWS
        query_tile_block = query_rows_list[start:stop]
        query_seg = query_tile_block.reshape(segments, CONT_LEN, heads_kv, head_group, depth)
        key_seg = key_rows_list[start:stop].reshape(segments, CONT_LEN, heads_kv, depth)
        value_seg = value_rows_list[start:stop].reshape(segments, CONT_LEN, heads_kv, depth)
        cross = (
            jnp.einsum(
                "rhgd,lhd->hgrl",
                query_tile_block,
                prompt_key_rows,
                preferred_element_type=jnp.float32,
            )
            * scale
        )
        own = (
            jnp.einsum("srhgd,slhd->hgsrl", query_seg, key_seg, preferred_element_type=jnp.float32)
            * scale
        )
        own_rows = jnp.where(causal, own, NEG_FILL).reshape(
            heads_kv, head_group, QUERY_BLOCK_ROWS, CONT_LEN
        )
        peak = jnp.maximum(
            jnp.max(cross, axis=-1, keepdims=True), jnp.max(own_rows, axis=-1, keepdims=True)
        )
        cross_raised = jnp.exp(cross - peak)
        own_raised = jnp.exp(own_rows - peak)
        total = jnp.sum(cross_raised, axis=-1, keepdims=True) + jnp.sum(
            own_raised, axis=-1, keepdims=True
        )
        cross_low = (cross_raised / total).astype(jnp.bfloat16)
        own_low = (
            (own_raised / total)
            .astype(jnp.bfloat16)
            .reshape(heads_kv, head_group, segments, CONT_LEN, CONT_LEN)
        )
        mixed_heads = jnp.einsum(
            "hgrl,lhd->rhgd", cross_low, prompt_value_rows, preferred_element_type=jnp.float32
        )
        mixed_heads = mixed_heads + jnp.einsum(
            "hgsrl,slhd->srhgd", own_low, value_seg, preferred_element_type=jnp.float32
        ).reshape(QUERY_BLOCK_ROWS, heads_kv, head_group, depth)
        mixed_parts.append(mixed_heads.astype(jnp.bfloat16).reshape(QUERY_BLOCK_ROWS, -1))
        lse_parts.append(peak + jnp.log(total))
    return (jnp.concatenate(mixed_parts, axis=0), jnp.stack(lse_parts))


def prompt_backward(
    query_rows_list,
    key_rows_list,
    value_rows_list,
    lse,
    upstream,
    prompt_key_rows,
    prompt_value_rows,
):
    scale = HEAD_SIZE ** (-0.5)
    query_parts = []
    key_grad = jnp.zeros(key_rows_list.shape, jnp.float32)
    value_grad = jnp.zeros(value_rows_list.shape, jnp.float32)
    for block in range(query_rows_list.shape[0] // QUERY_BLOCK_ROWS):
        start = block * QUERY_BLOCK_ROWS
        stop = start + QUERY_BLOCK_ROWS
        query_tile_block = query_rows_list[start:stop]
        up_block = upstream[start:stop]
        scores = (
            jnp.einsum(
                "rhgd,lhd->hgrl",
                query_tile_block,
                key_rows_list[:stop],
                preferred_element_type=jnp.float32,
            )
            * scale
        )
        allowed = jnp.arange(stop)[None, :] <= (start + jnp.arange(QUERY_BLOCK_ROWS))[:, None]
        scores = jnp.where(allowed, scores, NEG_FILL)
        probs = jnp.exp(scores - lse[block])
        prob_grad = jnp.einsum(
            "rhgd,lhd->hgrl", up_block, value_rows_list[:stop], preferred_element_type=jnp.float32
        )
        delta = jnp.sum(prob_grad * probs, axis=-1, keepdims=True)
        score_grad = (probs * (prob_grad - delta)).astype(jnp.bfloat16)
        query_parts.append(
            jnp.einsum(
                "hgrl,lhd->rhgd",
                score_grad,
                key_rows_list[:stop],
                preferred_element_type=jnp.float32,
            )
            * scale
        )
        key_grad = key_grad.at[:stop].add(
            jnp.einsum(
                "hgrl,rhgd->lhd", score_grad, query_tile_block, preferred_element_type=jnp.float32
            )
            * scale
        )
        value_grad = value_grad.at[:stop].add(
            jnp.einsum(
                "hgrl,rhgd->lhd",
                probs.astype(jnp.bfloat16),
                up_block,
                preferred_element_type=jnp.float32,
            )
        )
    empty = jnp.zeros(key_rows_list.shape, jnp.float32)
    return (jnp.concatenate(query_parts, axis=0), key_grad, value_grad, empty, empty)


def continuation_backward(
    query_rows_list,
    key_rows_list,
    value_rows_list,
    lse,
    upstream,
    prompt_key_rows,
    prompt_value_rows,
):
    heads_kv, head_group, depth = (
        query_rows_list.shape[1],
        query_rows_list.shape[2],
        query_rows_list.shape[3],
    )
    scale = HEAD_SIZE ** (-0.5)
    segments = QUERY_BLOCK_ROWS // CONT_LEN
    causal = jnp.arange(CONT_LEN)[None, :] <= jnp.arange(CONT_LEN)[:, None]
    query_parts = []
    near_keys = []
    near_values = []
    distant_key = jnp.zeros(prompt_key_rows.shape, jnp.float32)
    distant_value = jnp.zeros(prompt_value_rows.shape, jnp.float32)
    for block in range(query_rows_list.shape[0] // QUERY_BLOCK_ROWS):
        start = block * QUERY_BLOCK_ROWS
        stop = start + QUERY_BLOCK_ROWS
        query_tile_block = query_rows_list[start:stop]
        up_block = upstream[start:stop]
        query_seg = query_tile_block.reshape(segments, CONT_LEN, heads_kv, head_group, depth)
        up_seg = up_block.reshape(segments, CONT_LEN, heads_kv, head_group, depth)
        key_seg = key_rows_list[start:stop].reshape(segments, CONT_LEN, heads_kv, depth)
        value_seg = value_rows_list[start:stop].reshape(segments, CONT_LEN, heads_kv, depth)
        block_lse = lse[block]
        seg_lse = block_lse.reshape(heads_kv, head_group, segments, CONT_LEN, 1)
        cross = (
            jnp.einsum(
                "rhgd,lhd->hgrl",
                query_tile_block,
                prompt_key_rows,
                preferred_element_type=jnp.float32,
            )
            * scale
        )
        own = (
            jnp.einsum("srhgd,slhd->hgsrl", query_seg, key_seg, preferred_element_type=jnp.float32)
            * scale
        )
        own = jnp.where(causal, own, NEG_FILL)
        cross_probs = jnp.exp(cross - block_lse)
        own_probs = jnp.exp(own - seg_lse)
        cross_pgrad = jnp.einsum(
            "rhgd,lhd->hgrl", up_block, prompt_value_rows, preferred_element_type=jnp.float32
        )
        own_pgrad = jnp.einsum(
            "srhgd,slhd->hgsrl", up_seg, value_seg, preferred_element_type=jnp.float32
        )
        delta = jnp.sum(cross_pgrad * cross_probs, axis=-1, keepdims=True) + jnp.sum(
            own_pgrad * own_probs, axis=-1, keepdims=True
        ).reshape(heads_kv, head_group, QUERY_BLOCK_ROWS, 1)
        cross_sgrad = (cross_probs * (cross_pgrad - delta)).astype(jnp.bfloat16)
        own_sgrad = (
            own_probs * (own_pgrad - delta.reshape(heads_kv, head_group, segments, CONT_LEN, 1))
        ).astype(jnp.bfloat16)
        query_part = jnp.einsum(
            "hgrl,lhd->rhgd", cross_sgrad, prompt_key_rows, preferred_element_type=jnp.float32
        )
        query_part = query_part + jnp.einsum(
            "hgsrl,slhd->srhgd", own_sgrad, key_seg, preferred_element_type=jnp.float32
        ).reshape(QUERY_BLOCK_ROWS, heads_kv, head_group, depth)
        query_parts.append(query_part * scale)
        distant_key = (
            distant_key
            + jnp.einsum(
                "hgrl,rhgd->lhd", cross_sgrad, query_tile_block, preferred_element_type=jnp.float32
            )
            * scale
        )
        distant_value = distant_value + jnp.einsum(
            "hgrl,rhgd->lhd",
            cross_probs.astype(jnp.bfloat16),
            up_block,
            preferred_element_type=jnp.float32,
        )
        near_keys.append(
            (
                jnp.einsum(
                    "hgsrl,srhgd->slhd", own_sgrad, query_seg, preferred_element_type=jnp.float32
                )
                * scale
            ).reshape(QUERY_BLOCK_ROWS, heads_kv, depth)
        )
        near_values.append(
            jnp.einsum(
                "hgsrl,srhgd->slhd",
                own_probs.astype(jnp.bfloat16),
                up_seg,
                preferred_element_type=jnp.float32,
            ).reshape(QUERY_BLOCK_ROWS, heads_kv, depth)
        )
    return (
        jnp.concatenate(query_parts, axis=0),
        distant_key,
        distant_value,
        jnp.concatenate(near_keys, axis=0),
        jnp.concatenate(near_values, axis=0),
    )


def body(
    tokens,
    attn_gain,
    mlp_gain,
    query_weight,
    key_matrix,
    value_matrix,
    output_weight,
    gate_weight,
    up_weight,
    down_weight,
    cotangent,
):
    groups = lax.axis_size("grp")
    members = lax.axis_size("mem")
    shards = (
        attn_gain[None],
        mlp_gain[None],
        query_weight[None],
        key_matrix[None],
        value_matrix[None],
        output_weight[None],
        gate_weight[None],
        up_weight[None],
        down_weight[None],
    )
    gathered = (
        lax.all_gather(shards[0], ("grp", "mem"), axis=0, tiled=True),
        lax.all_gather(shards[1], ("grp", "mem"), axis=0, tiled=True),
        lax.all_gather(shards[2], ("grp", "mem"), axis=0, tiled=True),
        lax.all_gather(shards[3], ("grp", "mem"), axis=0, tiled=True),
        lax.all_gather(shards[4], ("grp", "mem"), axis=0, tiled=True),
        lax.all_gather(shards[5], ("grp", "mem"), axis=0, tiled=True),
        lax.all_gather(shards[6], ("grp", "mem"), axis=0, tiled=True),
        lax.all_gather(shards[7], ("grp", "mem"), axis=0, tiled=True),
        lax.all_gather(shards[8], ("grp", "mem"), axis=0, tiled=True),
    )
    gain_one, gain_two, matrices = unpack(gathered, groups, members)
    full_query, complete_key, full_value, complete_output, full_gate, full_up, full_down = matrices
    prompt_flag = lax.axis_index("mem") == 0
    rows_x = tokens[0].astype(jnp.float32)
    row_count = rows_x.shape[0]
    head_group = QUERY_HEADS // KEY_VALUE_HEADS
    local = jnp.arange(row_count)
    token_positions = jnp.where(prompt_flag, local, row_count + local % CONT_LEN)
    cosine_table, sine_table = rope_tables(token_positions)
    normalized_rows, inverse_one = norm_forward(rows_x, gain_one)
    query_rows_list = (
        rotary_apply(
            matrix_product(normalized_rows, full_query).reshape(row_count, QUERY_HEADS, HEAD_SIZE),
            cosine_table,
            sine_table,
            1.0,
        )
        .astype(jnp.bfloat16)
        .reshape(row_count, KEY_VALUE_HEADS, head_group, HEAD_SIZE)
    )
    flattened_keys = (
        rotary_apply(
            matrix_product(normalized_rows, complete_key).reshape(
                row_count, KEY_VALUE_HEADS, HEAD_SIZE
            ),
            cosine_table,
            sine_table,
            1.0,
        )
        .astype(jnp.bfloat16)
        .reshape(row_count, KEY_VALUE_HEADS * HEAD_SIZE)
    )
    flattened_values = matrix_product(normalized_rows, full_value).astype(jnp.bfloat16)
    common_keys, common_values = (
        broadcast(flattened_keys, "mem", 0),
        broadcast(flattened_values, "mem", 0),
    )
    key_rows_list = flattened_keys.reshape(row_count, KEY_VALUE_HEADS, HEAD_SIZE)
    value_rows_list = flattened_values.reshape(row_count, KEY_VALUE_HEADS, HEAD_SIZE)
    prompt_key_rows = common_keys.reshape(-1, KEY_VALUE_HEADS, HEAD_SIZE)
    prompt_value_rows = common_values.reshape(-1, KEY_VALUE_HEADS, HEAD_SIZE)
    mixed_heads, lse = lax.cond(
        prompt_flag,
        prompt_forward,
        continuation_forward,
        query_rows_list,
        key_rows_list,
        value_rows_list,
        prompt_key_rows,
        prompt_value_rows,
    )
    middle = rows_x + matrix_product(mixed_heads, complete_output)
    normed_two, inverse_two = norm_forward(middle, gain_two)
    gate_pre = matrix_product(normed_two, full_gate)
    up_pre = matrix_product(normed_two, full_up)
    sigma = jax.nn.sigmoid(gate_pre)
    hidden = (gate_pre * sigma * up_pre).astype(jnp.bfloat16)
    output = (middle + matrix_product(hidden, full_down)).astype(jnp.bfloat16)[None]
    refetched = (
        lax.all_gather(shards[0], ("grp", "mem"), axis=0, tiled=True),
        lax.all_gather(shards[1], ("grp", "mem"), axis=0, tiled=True),
        lax.all_gather(shards[2], ("grp", "mem"), axis=0, tiled=True),
        lax.all_gather(shards[3], ("grp", "mem"), axis=0, tiled=True),
        lax.all_gather(shards[4], ("grp", "mem"), axis=0, tiled=True),
        lax.all_gather(shards[5], ("grp", "mem"), axis=0, tiled=True),
        lax.all_gather(shards[6], ("grp", "mem"), axis=0, tiled=True),
        lax.all_gather(shards[7], ("grp", "mem"), axis=0, tiled=True),
        lax.all_gather(shards[8], ("grp", "mem"), axis=0, tiled=True),
    )
    gain_one, gain_two, matrices = unpack(refetched, groups, members)
    full_query, complete_key, full_value, complete_output, full_gate, full_up, full_down = matrices
    upstream = cotangent[0]
    down_wgrad = matmul_tn(hidden, upstream)
    hidden_grad = matrix_product_transposed(upstream, full_down)
    gate_grad = (hidden_grad * up_pre * sigma * (1.0 + gate_pre * (1.0 - sigma))).astype(
        jnp.bfloat16
    )
    up_grad = (hidden_grad * gate_pre * sigma).astype(jnp.bfloat16)
    gate_wgrad = matmul_tn(normed_two, gate_grad)
    up_wgrad = matmul_tn(normed_two, up_grad)
    normed_two_grad = matrix_product_transposed(gate_grad, full_gate) + matrix_product_transposed(
        up_grad, full_up
    )
    middle_norm_grad, gain_two_grad = norm_backward(
        middle, inverse_two, gain_two.astype(jnp.float32), normed_two_grad
    )
    middle_grad = upstream.astype(jnp.float32) + middle_norm_grad
    middle_lower_precision = middle_grad.astype(jnp.bfloat16)
    output_wgrad = matmul_tn(mixed_heads, middle_lower_precision)
    mixed_grad = (
        matrix_product_transposed(middle_lower_precision, complete_output)
        .astype(jnp.bfloat16)
        .reshape(row_count, KEY_VALUE_HEADS, head_group, HEAD_SIZE)
    )
    query_turned, distant_key, distant_value, nearby_key, nearby_value = lax.cond(
        prompt_flag,
        prompt_backward,
        continuation_backward,
        query_rows_list,
        key_rows_list,
        value_rows_list,
        lse,
        mixed_grad,
        prompt_key_rows,
        prompt_value_rows,
    )
    accumulated_key, accumulated_value = (
        lax.psum(
            distant_key.reshape(row_count, KEY_VALUE_HEADS * HEAD_SIZE).astype(jnp.bfloat16), "mem"
        ).astype(jnp.float32),
        lax.psum(
            distant_value.reshape(row_count, KEY_VALUE_HEADS * HEAD_SIZE).astype(jnp.bfloat16),
            "mem",
        ).astype(jnp.float32),
    )
    rotated_key = jnp.where(
        prompt_flag, accumulated_key, nearby_key.reshape(row_count, KEY_VALUE_HEADS * HEAD_SIZE)
    )
    value_total_sum = jnp.where(
        prompt_flag, accumulated_value, nearby_value.reshape(row_count, KEY_VALUE_HEADS * HEAD_SIZE)
    )
    query_raw = (
        rotary_apply(
            query_turned.reshape(row_count, QUERY_HEADS, HEAD_SIZE), cosine_table, sine_table, -1.0
        )
        .astype(jnp.bfloat16)
        .reshape(row_count, QUERY_HEADS * HEAD_SIZE)
    )
    key_raw = (
        rotary_apply(
            rotated_key.reshape(row_count, KEY_VALUE_HEADS, HEAD_SIZE),
            cosine_table,
            sine_table,
            -1.0,
        )
        .astype(jnp.bfloat16)
        .reshape(row_count, KEY_VALUE_HEADS * HEAD_SIZE)
    )
    value_raw = value_total_sum.astype(jnp.bfloat16)
    query_wgrad = matmul_tn(normalized_rows, query_raw)
    key_wgrad = matmul_tn(normalized_rows, key_raw)
    value_wgrad = matmul_tn(normalized_rows, value_raw)
    normed_grad = (
        matrix_product_transposed(query_raw, full_query)
        + matrix_product_transposed(key_raw, complete_key)
        + matrix_product_transposed(value_raw, full_value)
    )
    rows_norm_grad, gain_one_grad = norm_backward(
        rows_x, inverse_one, gain_one.astype(jnp.float32), normed_grad
    )
    tokens_grad = (middle_grad + rows_norm_grad).astype(jnp.bfloat16)[None]
    terms = (
        tile_gain(gain_one_grad, groups, members),
        tile_gain(gain_two_grad, groups, members),
        disperse(query_wgrad, groups, members),
        disperse(key_wgrad, groups, members),
        disperse(value_wgrad, groups, members),
        disperse(output_wgrad, groups, members),
        disperse(gate_wgrad, groups, members),
        disperse(up_wgrad, groups, members),
        disperse(down_wgrad, groups, members),
    )
    reduced = (
        lax.psum_scatter(terms[0], ("grp", "mem"), scatter_dimension=0, tiled=True),
        lax.psum_scatter(terms[1], ("grp", "mem"), scatter_dimension=0, tiled=True),
        lax.psum_scatter(terms[2], ("grp", "mem"), scatter_dimension=0, tiled=True),
        lax.psum_scatter(terms[3], ("grp", "mem"), scatter_dimension=0, tiled=True),
        lax.psum_scatter(terms[4], ("grp", "mem"), scatter_dimension=0, tiled=True),
        lax.psum_scatter(terms[5], ("grp", "mem"), scatter_dimension=0, tiled=True),
        lax.psum_scatter(terms[6], ("grp", "mem"), scatter_dimension=0, tiled=True),
        lax.psum_scatter(terms[7], ("grp", "mem"), scatter_dimension=0, tiled=True),
        lax.psum_scatter(terms[8], ("grp", "mem"), scatter_dimension=0, tiled=True),
    )
    return (
        output,
        tokens_grad,
        reduced[0][0],
        reduced[1][0],
        reduced[2][0],
        reduced[3][0],
        reduced[4][0],
        reduced[5][0],
        reduced[6][0],
        reduced[7][0],
        reduced[8][0],
    )


def solution(mesh):
    placed = (
        P("grp", "mem", None),
        P("mem"),
        P("mem"),
        P("grp", "mem"),
        P("grp", "mem"),
        P("grp", "mem"),
        P("grp", "mem"),
        P("grp", "mem"),
        P("grp", "mem"),
        P("grp", "mem"),
        P("grp", "mem", None),
    )
    return jax.shard_map(
        body,
        mesh=mesh,
        in_specs=placed,
        out_specs=(
            P("grp", "mem", None),
            P("grp", "mem", None),
            P("mem"),
            P("mem"),
            P("grp", "mem"),
            P("grp", "mem"),
            P("grp", "mem"),
            P("grp", "mem"),
            P("grp", "mem"),
            P("grp", "mem"),
            P("grp", "mem"),
        ),
        check_vma=False,
    )
```

profile of v0, /device:TPU:0, one launch (start us, length us, event | category | flops | bytes accessed | tf_op | source)
XLA Modules:
  0.0 1953.7 jit_solution(4727293989593099955)
XLA Ops:
  9.6 48.2 %all-gather.2 = bf16[4608,96]{1,0:T(8,128)(2,1)S(1)} all-gather(bf16[144,96]{1,0:T(8,128)(2,1)} %param.31), channel_id=4, replica_groups=mesh['grp'=8,'mem'=4] {'grp','mem'}, dimensions={0}, use_global_device_ids=true | all-gather | bytes 912384 | tf_op jit(solution)/shard_map/all_gather | solution.py:397
  64.5 41.1 %all-gather.3 = bf16[4608,96]{1,0:T(8,128)(2,1)S(1)} all-gather(bf16[144,96]{1,0:T(8,128)(2,1)S(1)} %copy-done.66), channel_id=5, replica_groups=mesh['grp'=8,'mem'=4] {'grp','mem'}, dimensions={0}, use_global_device_ids=true | all-gather | bytes 912384 | tf_op jit(solution)/shard_map/all_gather | solution.py:398
  110.4 38.4 %all-reduce.7 = (bf16[9216]{0:T(1024)(128)(2,1)S(1)}, bf16[9216]{0:T(1024)(128)(2,1)S(1)}) all-reduce(bf16[9216]{0:T(1024)(128)(2,1)S(1)} %dynamic-update-slice.12, bf16[9216]{0:T(1024)(128)(2,1)S(1)} %dynamic-update-slice.13), channel_id=2, replica_groups=mesh['grp'=8,'mem'=4] {'grp','mem'}, use_global_device_ids=true, to_apply=%add.2 | all-reduce | flops 18432 | bytes 73728
  160.5 5.3 copy.514
  165.8 6.5 reshape.836
  172.3 5.3 copy.513
  177.5 6.4 reshape.845
  184.0 5.2 copy.230
  189.2 5.4 fusion.271
  197.1 9.4 all-reduce.18.cloned.1.call-done
  206.5 93.7 %conditional.2 = (bf16[1024,1152]{0,1:T(8,128)(2,1)S(1)}, f32[2,6,3,512,1]{3,2,1,4,0:T(4,128)}) conditional(s32[]{:T(128)} %convert_element_type.234, (bf16[1024,6,3,64]{0,3,2,1:T(8,128)(2,1)}, bf16[1024,6,64]{0,2,1:T(8,128)(2,1)}, bf16[1024,6,64]{0,2,1:T(8,128)(2,1)S(1)}, bf16[1024,6,64]{0,2,1:T(8,128)(2,1)}, ...), branch_computations={%region_3.12_spmd, %region_12.17_spmd} | conditional | flops 5641166848 | bytes 462577856 | solution.py:445
  216.9 9.3 fusion.50
  226.2 10.3 fusion.49
  236.5 10.0 fusion.52
  246.5 16.3 fusion.47
  262.8 16.7 fusion.46
  279.5 17.9 fusion.53
  300.3 6.7 multiply_reduce_fusion.2
  311.1 9.5 copy.235
  320.6 7.7 copy.382
  328.2 10.0 copy.236
  338.2 7.6 copy.383
  345.8 39.0 %all-gather.23.cloned.1.call-done = bf16[12288,288]{0,1:T(8,128)(2,1)} async-done(((bf16[384,288]{0,1:T(8,128)(2,1)}), bf16[12288,288]{0,1:T(8,128)(2,1)}) %all-gather.23.cloned.1.call-update) | async-done | bytes 7077904 | tf_op jit(solution)/shard_map/all_gather | solution.py:402
  384.8 11.7 reshape.850
  405.3 12.6 fusion.297
  417.9 18.4 fusion.240
  436.3 20.3 %multiply_convert_fusion = (bf16[1024,3072]{1,0:T(8,128)(2,1)}, bf16[1024,3072]{1,0:T(8,128)(2,1)}) fusion(f32[1024,3072]{1,0:T(8,128)} %fusion.297, f32[1024,3072]{1,0:T(8,128)} %get-tuple-element.369, bf16[3072,1152]{0,1:T(8,128)(2,1)} %bitcast.898, bf16[1,1024,1152]{2,1,0:T(8,128)(2,1)S(1)} %copy-done.17), kind=kOutput, calls=%fused_computation.309 | convolution fusion | flops 7288651776 | bytes 47185920 | tf_op jit(solution)/shard_map/dot_general | solution.py:33
  456.7 14.2 fusion.298
  470.9 15.3 multiply_reduce_fusion
  498.5 184.8 %conditional.3 = (bf16[1024,6,64]{0,2,1:T(8,128)(2,1)}, bf16[1024,6,64]{0,2,1:T(8,128)(2,1)}, f32[1024,384]{0,1:T(8,128)}, f32[1024,384]{0,1:T(8,128)}, f32[1024...) conditional(s32[]{:T(128)} %convert_element_type.234, (bf16[1024,6,3,64]{0,3,2,1:T(8,128)(2,1)}, ...), branch_computations={%region_19.24_spmd.clone.clone, %region_24.27_spmd.clone.clone} | conditional | flops 13851049984 | bytes 939245824 | solution.py:498
  509.7 9.1 fusion.225
  518.8 9.6 fusion.210
  528.4 13.0 fusion.196
  541.5 13.5 fusion.198
  555.0 5.1 fusion.214
  563.2 16.0 fusion.219
  579.3 17.1 bitcast_add_fusion.16
  596.4 30.9 %fusion.190 = (f32[6,3,512]{2,1,0:T(4,128)S(1)}, f32[6,1024,512,3]{2,1,3,0:T(8,128)}) fusion(f32[6,1024,512,3]{2,1,3,0:T(8,128)} %fusion.219, f32[6,3,512]{2,1,0:T(4,128)S(1)} %get-tuple-element.337, pred[512,1024]{0,1:T(8,128)(4,1)} %iota_compare_fusion.4, bf16[1024,6,3,64]{0,3,2,1:T(8,128)(2,1)S(1)} %get-tuple-element.258, ...), kind=kOutput, calls=%fused_computation.242 | convolution fusion | flops 1255136256 | bytes 78073856 | tf_op jit(solution)/shard_map/cond/branch_1_fun/rhgd,lhd->hgrl/dot_general | solution.py:228
  627.3 30.9 %fusion.192 = bf16[6,3,512,1024]{2,3,1,0:T(8,128)(2,1)} fusion(f32[6,1024,512,3]{2,1,3,0:T(8,128)} %get-tuple-element.342, f32[6,1024,512,3]{2,1,3,0:T(8,128)} %fusion.219, f32[6,3,512]{2,1,0:T(4,128)S(1)} %get-tuple-element.341, f32[6,3,512]{2,1,0:T(4,128)S(1)} %get-tuple-element.337, pred[512,1024]{0,1:T(8,128)(4,1)} %iota_compare_fusion.4), kind=kLoop, calls=%fused_computation.244 | loop fusion | flops 56623104 | bytes 94969856 | tf_op jit(solution)/shard_map/cond/branch_1_fun/convert_element_type | solution.py:232
  658.2 10.6 bitcast_add_fusion.17
  668.8 8.3 multiply_bitcast_fusion
  688.5 5.2 fusion.299
  693.7 141.8 %all-reduce.16.cloned.1.call-done = (bf16[1024,384]{0,1:T(8,128)(2,1)}, bf16[1024,384]{0,1:T(8,128)(2,1)}) async-done(((bf16[1024,384]{0,1:T(8,128)(2,1)}, bf16[1024,384]{0,1:T(8,128)(2,1)}), (bf16[1024,384]{0,1:T(8,128)(2,1)}, bf16[1024,384]{0,1:T(8,128)(2,1)})) %all-reduce.16.cloned.1.call-update) | async-done | bytes 1572880 | tf_op jit(solution)/shard_map/psum | solution.py:511
  845.0 6.2 fusion.265
  865.2 7.3 fusion.278
  872.6 8.6 reshape.859
  881.1 6.6 copy.241
  889.4 7.5 fusion.300
  901.1 8.8 copy.316
  909.9 12.6 fusion.305
  924.2 13.0 fusion.304
  937.1 18.2 reshape.863
  955.3 12.6 copy.243
  968.2 13.0 fusion.303
  981.1 18.2 reshape.861
  999.4 12.7 copy.242
  1012.1 19.1 fusion.264
  1033.8 53.7 %reduce-scatter.12.cloned.1.call-done = f32[1,144,96]{2,1,0:T(8,128)} async-done(((f32[32,144,96]{2,1,0:T(8,128)}), f32[1,144,96]{2,1,0:T(8,128)}) %reduce-scatter.12.cloned.1.call-update) | async-done | bytes 55312 | tf_op jit(solution)/shard_map/reduce_scatter | solution.py:571
  1087.4 104.5 %reduce-scatter.10.cloned.1.call-done = f32[1,144,96]{2,1,0:T(8,128)} async-done(((f32[32,144,96]{2,1,0:T(8,128)}), f32[1,144,96]{2,1,0:T(8,128)}) %reduce-scatter.10.cloned.1.call-update) | async-done | bytes 55312 | tf_op jit(solution)/shard_map/reduce_scatter | solution.py:570
  1192.0 124.8 %reduce-scatter.14.cloned.1.call-done = f32[1,144,288]{2,1,0:T(8,128)} async-done(((f32[32,144,288]{2,1,0:T(8,128)}), f32[1,144,288]{2,1,0:T(8,128)}) %reduce-scatter.14.cloned.1.call-update) | async-done | bytes 165904 | tf_op jit(solution)/shard_map/reduce_scatter | solution.py:572
  1316.8 124.7 %reduce-scatter.8.cloned.1.call-done = f32[1,144,288]{2,1,0:T(8,128)} async-done(((f32[32,144,288]{2,1,0:T(8,128)}), f32[1,144,288]{2,1,0:T(8,128)}) %reduce-scatter.8.cloned.1.call-update) | async-done | bytes 165904 | tf_op jit(solution)/shard_map/reduce_scatter | solution.py:569
  1441.5 168.2 %reduce-scatter.20.cloned.1.call-done = f32[1,384,288]{1,2,0:T(8,128)} async-done(((f32[32,384,288]{1,2,0:T(8,128)}), f32[1,384,288]{1,2,0:T(8,128)}) %reduce-scatter.20.cloned.1.call-update) | async-done | bytes 442384 | tf_op jit(solution)/shard_map/reduce_scatter | solution.py:575
  1609.7 168.6 %reduce-scatter.18.cloned.1.call-done = f32[1,144,768]{2,1,0:T(8,128)} async-done(((f32[32,144,768]{2,1,0:T(8,128)}), f32[1,144,768]{2,1,0:T(8,128)}) %reduce-scatter.18.cloned.1.call-update) | async-done | bytes 442384 | tf_op jit(solution)/shard_map/reduce_scatter | solution.py:574
  1778.3 168.1 %reduce-scatter.16.cloned.1.call-done = f32[1,144,768]{2,1,0:T(8,128)} async-done(((f32[32,144,768]{2,1,0:T(8,128)}), f32[1,144,768]{2,1,0:T(8,128)}) %reduce-scatter.16.cloned.1.call-update) | async-done | bytes 442384 | tf_op jit(solution)/shard_map/reduce_scatter | solution.py:573
  (194 shorter events, 106.0 us)
Async XLA Ops:
  8.0 56.4 %copy-start.66 = (bf16[144,96]{1,0:T(8,128)(2,1)S(1)}, bf16[144,96]{1,0:T(8,128)(2,1)}, u32[]{:S(2)}) copy-start(bf16[144,96]{1,0:T(8,128)(2,1)} %param.32) | copy-start | bytes 82948
  8.0 152.4 %all-gather.15.cloned.1.call-start = ((), (), s32[]{:S(2)}) async-start(), calls=%async_computation.14 | async-start | bytes 3649536 | tf_op jit(solution)/shard_map/all_gather | solution.py:396
  8.8 163.5 %all-gather.17.cloned.1.call-start = ((), (), s32[]{:S(2)}) async-start(), calls=%async_computation.15 | async-start | bytes 3649536 | tf_op jit(solution)/shard_map/all_gather | solution.py:399
  9.5 197.0 %all-reduce.18.cloned.1.call-start = ((), (), s32[]{:S(2)}) async-start(), calls=%async_computation.21 | async-start | bytes 3145728 | tf_op jit(solution)/shard_map/psum | solution.py:19
  59.2 50.6 %copy-start.70 = (bf16[288]{0:T(512)(128)(2,1)S(1)}, bf16[288]{0:T(512)(128)(2,1)}, u32[]{:S(2)}) copy-start(bf16[288]{0:T(512)(128)(2,1)} %param.28) | copy-start | bytes 1732
  59.2 50.9 %copy-start.71 = (bf16[288]{0:T(512)(128)(2,1)S(1)}, bf16[288]{0:T(512)(128)(2,1)}, u32[]{:S(2)}) copy-start(bf16[288]{0:T(512)(128)(2,1)} %param.29) | copy-start | bytes 1732
  59.2 89.6 %copy-start.9 = (bf16[1,1024,1152]{2,1,0:T(8,128)(2,1)S(1)}, bf16[1,1024,1152]{2,1,0:T(8,128)(2,1)}, u32[]{:S(2)}) copy-start(bf16[1,1024,1152]{2,1,0:T(8,128)(2,1)} %param.27) | copy-start | bytes 7077892
  150.0 39.2 %copy-start.67 = (f32[1024]{0:T(1024)}, f32[1024]{0:T(1024)S(1)}, u32[]{:S(2)}) copy-start(f32[1024]{0:T(1024)S(1)} %get-tuple-element.359) | copy-start | bytes 12292
  150.6 38.6 %copy-start.63 = (f32[1152]{0:T(1024)}, f32[1152]{0:T(1024)S(1)}, u32[]{:S(2)}) copy-start(f32[1152]{0:T(1024)S(1)} %get-tuple-element.371) | copy-start | bytes 13828
  151.8 42.8 %copy-start.37 = (f32[1024,32]{0,1:T(8,128)}, f32[1024,32]{0,1:T(8,128)S(1)}, u32[]{:S(2)}) copy-start(f32[1024,32]{0,1:T(8,128)S(1)} %get-tuple-element.357) | copy-start | bytes 393220
  154.3 1.4 copy-start.31
  155.7 50.8 %copy-start.1 = (bf16[1024,6,64]{0,2,1:T(8,128)(2,1)}, bf16[1024,6,64]{0,2,1:T(8,128)(2,1)S(1)}, u32[]{:S(2)}) copy-start(bf16[1024,6,64]{0,2,1:T(8,128)(2,1)S(1)} %get-tuple-element.282) | copy-start | bytes 2359300
  158.3 152.8 %all-gather.19.cloned.1.call-start = ((), (), s32[]{:S(2)}) async-start(), calls=%async_computation.16 | async-start | bytes 7299072 | tf_op jit(solution)/shard_map/all_gather | solution.py:400
  159.0 169.2 %all-gather.21.cloned.1.call-start = ((), (), s32[]{:S(2)}) async-start(), calls=%async_computation.17 | async-start | bytes 7299072 | tf_op jit(solution)/shard_map/all_gather | solution.py:401
  159.6 225.2 %all-gather.23.cloned.1.call-start = ((), (), s32[]{:S(2)}) async-start(), calls=%async_computation.18 | async-start | bytes 7299072 | tf_op jit(solution)/shard_map/all_gather | solution.py:402
  160.2 675.3 %all-reduce.16.cloned.1.call-start = ((), (), s32[]{:S(2)}) async-start(), calls=%async_computation.20 | async-start | bytes 3145728 | tf_op jit(solution)/shard_map/psum | solution.py:511
  206.5 93.7 %copy-start.10 = (bf16[1,1024,1152]{2,1,0:T(8,128)(2,1)S(1)}, bf16[1,1024,1152]{2,1,0:T(8,128)(2,1)}, u32[]{:S(2)}) copy-start(bf16[1,1024,1152]{2,1,0:T(8,128)(2,1)} %param.27) | copy-start | bytes 7077892
  236.5 10.0 copy-start.20
  262.8 16.7 copy-start.14
  300.2 6.8 copy-start.47
  300.2 9.0 copy-start.65
  307.0 2.2 copy-start.12
  396.5 8.8 slice-start.7
  400.6 4.7 slice-start.8
  405.3 12.6 copy-start.50
  417.9 18.4 copy-start.17
  456.7 29.5 %slice-start.5 = ((s8[4718592]{0:T(1024)(128)(4,1)}), s8[4194304]{0:T(1024)(128)(4,1)S(1)}, s32[]{:S(2)}) async-start(s8[4718592]{0:T(1024)(128)(4,1)} %bitcast.886), calls=%async_computation.27 | async-start | bytes 8388608
  470.9 15.3 slice-start.6
  486.2 3.9 copy-start.42
  488.0 2.1 copy-start.13
  494.9 3.0 copy-start.2
  563.2 16.0 copy-start.6
  563.2 16.0 copy-start.72
  627.3 30.9 %copy-start.56 = (f32[512,6,64]{0,2,1:T(8,128)S(1)}, f32[512,6,64]{0,2,1:T(8,128)}, u32[]{:S(2)}) copy-start(f32[512,6,64]{0,2,1:T(8,128)} %fusion.214) | copy-start | bytes 2359300 | tf_op jit(solution)/shard_map/cond
  668.8 8.3 copy-start.19
  683.4 347.8 %all-reduce.14.cloned.1.call-start = ((), (), s32[]{:S(2)}) async-start(), calls=%async_computation.19 | async-start | bytes 196608
  683.4 5.0 copy-start.15
  687.1 1.4 copy-start.45
  688.5 148.5 %copy-start.38 = (f32[1024,32]{0,1:T(8,128)S(1)}, f32[1024,32]{0,1:T(8,128)}, u32[]{:S(2)}) copy-start(f32[1024,32]{0,1:T(8,128)} %copy-done.37) | copy-start | bytes 393220
  688.5 148.6 %copy-start.54 = (f32[1024,32]{0,1:T(8,128)S(1)}, f32[1024,32]{0,1:T(8,128)}, u32[]{:S(2)}) copy-start(f32[1024,32]{0,1:T(8,128)} %get-tuple-element.355) | copy-start | bytes 393220
  835.5 1.8 copy-start.55
  835.5 3.0 copy-start.21
  835.5 3.1 copy-start.30
  837.6 0.9 copy-start.40
  838.6 1.7 copy-start.11
  838.6 1.9 copy-start.32
  838.6 1.9 copy-start.64
  838.6 1.9 copy-start.68
  840.5 4.5 copy-start.69
  855.5 231.9 %reduce-scatter.12.cloned.1.call-start = ((), (), s32[]{:S(2)}) async-start(), calls=%async_computation.9 | async-start | bytes 2433024 | tf_op jit(solution)/shard_map/reduce_scatter | solution.py:571
  855.6 4.7 copy-start.41
  860.2 331.8 %reduce-scatter.10.cloned.1.call-start = ((), (), s32[]{:S(2)}) async-start(), calls=%async_computation.8 | async-start | bytes 2433024 | tf_op jit(solution)/shard_map/reduce_scatter | solution.py:570
  860.2 5.0 copy-start.48
  865.0 451.8 %reduce-scatter.14.cloned.1.call-start = ((), (), s32[]{:S(2)}) async-start(), calls=%async_computation.10 | async-start | bytes 7299072 | tf_op jit(solution)/shard_map/reduce_scatter | solution.py:572
  887.7 1.7 copy-start.46
  887.7 553.7 %reduce-scatter.8.cloned.1.call-start = ((), (), s32[]{:S(2)}) async-start(), calls=%async_computation.7 | async-start | bytes 7299072 | tf_op jit(solution)/shard_map/reduce_scatter | solution.py:569
  896.9 1.7 copy-start.18
  896.9 712.7 %reduce-scatter.20.cloned.1.call-start = ((), (), s32[]{:S(2)}) async-start(), calls=%async_computation.13 | async-start | bytes 14598144 | tf_op jit(solution)/shard_map/reduce_scatter | solution.py:575
  901.1 8.8 copy-start.49
  922.5 1.7 copy-start.51
  922.5 855.8 %reduce-scatter.18.cloned.1.call-start = ((), (), s32[]{:S(2)}) async-start(), calls=%async_computation.12 | async-start | bytes 14598144 | tf_op jit(solution)/shard_map/reduce_scatter | solution.py:574
  967.9 978.5 %reduce-scatter.16.cloned.1.call-start = ((), (), s32[]{:S(2)}) async-start(), calls=%async_computation.11 | async-start | bytes 14598144 | tf_op jit(solution)/shard_map/reduce_scatter | solution.py:573
Sparse Core Ops, SparseCore 0:
  11.7 65.5 all-gather.14
  80.2 58.4 all-gather.16
  162.0 74.6 all-gather.18
  239.5 70.5 all-gather.20
  312.9 71.8 all-gather.22
  855.6 125.2 all-reduce.13
  986.8 100.5 reduce-scatter.11
  1093.3 98.6 reduce-scatter.9
  1198.2 118.5 reduce-scatter.13
  1322.9 118.5 reduce-scatter.7
  1448.0 161.5 reduce-scatter.19
  1616.1 162.1 reduce-scatter.17
  1784.9 161.4 reduce-scatter.15
Sparse Core Ops, SparseCore 1:
  158.4 48.1 all-reduce.17
  683.5 151.9 all-reduce.15
where the time goes:
time: 1960 us; the launch traced here: 1950 us
  waiting for transfers between devices  1110 us (57%)
  matrix products  371 us (19%)
  local copies, waits for them, and re-layouts  213 us (11%)
  blocking collectives  128 us (7%)
  other arithmetic  99.3 us (5%)
    reduce_scatter x1, waiting for transfers between devices, body(): lax.psum_scatter(terms[7], ('grp', 'mem'), scatter_dimension=0, tiled=True)  169 us
    reduce_scatter x1, waiting for transfers between devices, body(): lax.psum_scatter(terms[8], ('grp', 'mem'), scatter_dimension=0, tiled=True)  168 us
    reduce_scatter x1, waiting for transfers between devices, body(): lax.psum_scatter(terms[6], ('grp', 'mem'), scatter_dimension=0, tiled=True)  168 us
    psum x1, waiting for transfers between devices, body(): lax.psum(distant_key.reshape(row_count, KEY_VALUE_HEADS * HEAD_SIZE).asty...  142 us
    reduce_scatter x1, waiting for transfers between devices, body(): lax.psum_scatter(terms[5], ('grp', 'mem'), scatter_dimension=0, tiled=True)  125 us
    reduce_scatter x1, waiting for transfers between devices, body(): lax.psum_scatter(terms[2], ('grp', 'mem'), scatter_dimension=0, tiled=True)  125 us
    reduce_scatter x1, waiting for transfers between devices, body(): lax.psum_scatter(terms[3], ('grp', 'mem'), scatter_dimension=0, tiled=True)  105 us
    dot_general x7, matrix products, matrix_product(): return jnp.dot(left, right, preferred_element_type=jnp.float32)  67.2 us
  transfers between devices with their start and end apart: 15, of which 10 were waited for; matrix products, arithmetic and copies ran while one was open for 19% of the time, Pallas kernels for 0%

commit v1 on v0

v1 whole, which is shorter than its diff:
```python
import functools

import jax
import jax.numpy as jnp
from jax import lax
from jax.experimental import pallas as pl
from jax.experimental.pallas import tpu as pltpu
from jax.sharding import PartitionSpec as P

QUERY_HEADS = 18
KEY_VALUE_HEADS = 6
HEAD_SIZE = 64
CONT_LEN = 128
EPSILON = 1e-05
NEG_FILL = -1e30
ROWS = 256
SCALE = HEAD_SIZE ** (-0.5)
F32 = jnp.float32
BF16 = jnp.bfloat16
VMEM_LIMIT = 56 * 2**20


def dot_nn(left, right):
    return lax.dot_general(left, right, (((1,), (0,)), ((), ())), preferred_element_type=F32)


def dot_nt(left, right):
    return lax.dot_general(left, right, (((1,), (1,)), ((), ())), preferred_element_type=F32)


def dot_tn(left, right):
    return lax.dot_general(left, right, (((0,), (0,)), ((), ())), preferred_element_type=F32)


def params(**more):
    return pltpu.CompilerParams(vmem_limit_bytes=VMEM_LIMIT, **more)


def turn(values, cosine, sine, direction):
    half = HEAD_SIZE // 2
    parts = []
    for head in range(values.shape[0] // HEAD_SIZE):
        first = values[head * HEAD_SIZE : head * HEAD_SIZE + half]
        second = values[head * HEAD_SIZE + half : (head + 1) * HEAD_SIZE]
        parts.append(first * cosine - direction * second * sine)
        parts.append(second * cosine + direction * first * sine)
    return jnp.concatenate(parts, axis=0)


def forward_kernel(flag_ref, q_ref, k_ref, v_ref, pk_ref, pv_ref, out_ref, lse_ref, kt_s, vt_s):
    step = pl.program_id(1)
    prompt = pk_ref.shape[0]

    @pl.when(step == 0)
    def _():
        for half in range(2):
            kt_s[half] = pk_ref[:, half * HEAD_SIZE : (half + 1) * HEAD_SIZE]
        vt_s[...] = pv_ref[...].T

    def heads(is_prompt):
        if is_prompt:
            key = lax.broadcasted_iota(jnp.int32, (prompt, ROWS), 0)
            row = lax.broadcasted_iota(jnp.int32, (prompt, ROWS), 1) + step * ROWS
            seen = key <= row
        else:
            key = lax.broadcasted_iota(jnp.int32, (ROWS, ROWS), 0)
            row = lax.broadcasted_iota(jnp.int32, (ROWS, ROWS), 1)
            seen = (key // CONT_LEN == row // CONT_LEN) & (key <= row)
            own_vt = v_ref[...].T
        per_pair = 2 * (QUERY_HEADS // KEY_VALUE_HEADS)
        outs = []
        for head in range(per_pair):
            kv = head // (per_pair // 2)
            span = slice(kv * HEAD_SIZE, (kv + 1) * HEAD_SIZE)
            q_t = q_ref[head * HEAD_SIZE : (head + 1) * HEAD_SIZE, :] * jnp.asarray(SCALE, BF16)
            scores = dot_nn(kt_s[kv], q_t)
            if is_prompt:
                scores = jnp.where(seen, scores, NEG_FILL)
                peak = jnp.max(scores, axis=0, keepdims=True)
                raised = jnp.exp(scores - peak)
                total = jnp.sum(raised, axis=0, keepdims=True)
                mixed = dot_nn(vt_s[span, :], raised.astype(BF16))
            else:
                own = jnp.where(seen, dot_nn(k_ref[:, span], q_t), NEG_FILL)
                peak = jnp.maximum(
                    jnp.max(scores, axis=0, keepdims=True), jnp.max(own, axis=0, keepdims=True)
                )
                raised = jnp.exp(scores - peak)
                own = jnp.exp(own - peak)
                total = jnp.sum(raised, axis=0, keepdims=True) + jnp.sum(
                    own, axis=0, keepdims=True
                )
                mixed = dot_nn(vt_s[span, :], raised.astype(BF16)) + dot_nn(
                    own_vt[span, :], own.astype(BF16)
                )
            outs.append(mixed / total)
            lse_ref[0, head : head + 1, :] = peak + jnp.log(total)
        out_ref[...] = jnp.concatenate(outs, axis=0).T.astype(BF16)

    @pl.when(flag_ref[0] == 1)
    def _():
        heads(True)

    @pl.when(flag_ref[0] == 0)
    def _():
        heads(False)


def attention_forward(flag, q_t, k, v, pk, pv):
    rows = k.shape[0]
    prompt = pk.shape[0]
    pairs = KEY_VALUE_HEADS // 2
    wide = q_t.shape[0] // pairs
    pair = 2 * HEAD_SIZE
    per_pair = wide // HEAD_SIZE
    return pl.pallas_call(
        forward_kernel,
        out_shape=(
            jax.ShapeDtypeStruct((rows, q_t.shape[0]), BF16),
            jax.ShapeDtypeStruct((pairs, 8, rows), F32),
        ),
        grid_spec=pltpu.PrefetchScalarGridSpec(
            num_scalar_prefetch=1,
            grid=(pairs, rows // ROWS),
            in_specs=[
                pl.BlockSpec((wide, ROWS), lambda p, i, f: (p, i)),
                pl.BlockSpec((ROWS, pair), lambda p, i, f: (i, p)),
                pl.BlockSpec((ROWS, pair), lambda p, i, f: (i, p)),
                pl.BlockSpec((prompt, pair), lambda p, i, f: (0, p)),
                pl.BlockSpec((prompt, pair), lambda p, i, f: (0, p)),
            ],
            out_specs=[
                pl.BlockSpec((ROWS, wide), lambda p, i, f: (i, p)),
                pl.BlockSpec((1, 8, ROWS), lambda p, i, f: (p, 0, i)),
            ],
            scratch_shapes=[
                pltpu.VMEM((2, prompt, HEAD_SIZE), BF16),
                pltpu.VMEM((pair, prompt), BF16),
            ],
        ),
        compiler_params=params(dimension_semantics=("arbitrary", "arbitrary")),
        name="attention_forward",
    )(flag, q_t, k, v, pk, pv)


def backward_kernel(
    flag_ref, q_ref, k_ref, v_ref, pk_ref, pv_ref, lse_ref, up_ref, mixed_ref, cos_ref, sin_ref,
    dq_ref, far_k_ref, far_v_ref, near_k_ref, near_v_ref, key_s, val_s, keyt_s,
):
    step = pl.program_id(1)
    prompt = pk_ref.shape[0]
    half_scale = jnp.asarray(SCALE, BF16)

    @pl.when(step == 0)
    def _():
        for half in range(2):
            key_s[half] = pk_ref[:, half * HEAD_SIZE : (half + 1) * HEAD_SIZE]
            val_s[half] = pv_ref[:, half * HEAD_SIZE : (half + 1) * HEAD_SIZE]
        keyt_s[...] = pk_ref[...].T * half_scale
        far_k_ref[...] = jnp.zeros_like(far_k_ref)
        far_v_ref[...] = jnp.zeros_like(far_v_ref)

    def heads(is_prompt):
        if is_prompt:
            key = lax.broadcasted_iota(jnp.int32, (prompt, ROWS), 0)
            row = lax.broadcasted_iota(jnp.int32, (prompt, ROWS), 1) + step * ROWS
            seen = key <= row
            near_k_ref[...] = jnp.zeros_like(near_k_ref)
            near_v_ref[...] = jnp.zeros_like(near_v_ref)
        else:
            key = lax.broadcasted_iota(jnp.int32, (ROWS, ROWS), 0)
            row = lax.broadcasted_iota(jnp.int32, (ROWS, ROWS), 1)
            seen = (key // CONT_LEN == row // CONT_LEN) & (key <= row)
            own_kt = k_ref[...].T * half_scale
        up = up_ref[...]
        up_t = up.T
        product_t = (up.astype(F32) * mixed_ref[...].astype(F32)).T
        per_pair = 2 * (QUERY_HEADS // KEY_VALUE_HEADS)
        turned = []
        far_k, far_v, near_k, near_v = [], [], [], []
        for kv in range(2):
            span = slice(kv * HEAD_SIZE, (kv + 1) * HEAD_SIZE)
            sums = None
            for inner in range(per_pair // 2):
                head = kv * (per_pair // 2) + inner
                place = slice(head * HEAD_SIZE, (head + 1) * HEAD_SIZE)
                q_t = q_ref[place, :] * half_scale
                q_n = q_t.T
                u_t = up_t[place, :]
                u_n = up[:, place]
                lse = lse_ref[0, head : head + 1, :]
                delta = jnp.sum(product_t[place, :], axis=0, keepdims=True)
                scores = dot_nn(key_s[kv], q_t)
                if is_prompt:
                    scores = jnp.where(seen, scores, NEG_FILL)
                probs = jnp.exp(scores - lse)
                grad = (probs * (dot_nn(val_s[kv], u_t) - delta)).astype(BF16)
                dq = dot_nn(keyt_s[span, :], grad)
                parts = [dot_nn(grad, q_n), dot_nn(probs.astype(BF16), u_n)]
                if not is_prompt:
                    own = jnp.where(seen, dot_nn(k_ref[:, span], q_t), NEG_FILL)
                    own = jnp.exp(own - lse)
                    own_grad = (own * (dot_nn(v_ref[:, span], u_t) - delta)).astype(BF16)
                    dq = dq + dot_nn(own_kt[span, :], own_grad)
                    parts += [dot_nn(own_grad, q_n), dot_nn(own.astype(BF16), u_n)]
                turned.append(dq)
                sums = parts if sums is None else [a + b for a, b in zip(sums, parts)]
            far_k.append(sums[0])
            far_v.append(sums[1])
            if not is_prompt:
                near_k.append(sums[2])
                near_v.append(sums[3])
        dq_ref[...] = (
            turn(jnp.concatenate(turned, axis=0), cos_ref[...], sin_ref[...], -1.0)
            .T.astype(BF16)
        )
        far_k_ref[...] += jnp.concatenate(far_k, axis=1)
        far_v_ref[...] += jnp.concatenate(far_v, axis=1)
        if not is_prompt:
            near_k_ref[...] = jnp.concatenate(near_k, axis=1)
            near_v_ref[...] = jnp.concatenate(near_v, axis=1)

    @pl.when(flag_ref[0] == 1)
    def _():
        heads(True)

    @pl.when(flag_ref[0] == 0)
    def _():
        heads(False)


def attention_backward(flag, q_t, k, v, pk, pv, lse, up, mixed, cosine, sine):
    rows = k.shape[0]
    prompt = pk.shape[0]
    pairs = KEY_VALUE_HEADS // 2
    wide = q_t.shape[0] // pairs
    pair = 2 * HEAD_SIZE
    near = pl.BlockSpec((ROWS, pair), lambda p, i, f: (i, p))
    far = pl.BlockSpec((prompt, pair), lambda p, i, f: (0, p))
    band = pl.BlockSpec((ROWS, wide), lambda p, i, f: (i, p))
    table = pl.BlockSpec((HEAD_SIZE // 2, ROWS), lambda p, i, f: (0, i))
    return pl.pallas_call(
        backward_kernel,
        out_shape=(
            jax.ShapeDtypeStruct((rows, q_t.shape[0]), BF16),
            jax.ShapeDtypeStruct(pk.shape, F32),
            jax.ShapeDtypeStruct(pv.shape, F32),
            jax.ShapeDtypeStruct(k.shape, F32),
            jax.ShapeDtypeStruct(v.shape, F32),
        ),
        grid_spec=pltpu.PrefetchScalarGridSpec(
            num_scalar_prefetch=1,
            grid=(pairs, rows // ROWS),
            in_specs=[
                pl.BlockSpec((wide, ROWS), lambda p, i, f: (p, i)),
                near, near, far, far,
                pl.BlockSpec((1, 8, ROWS), lambda p, i, f: (p, 0, i)),
                band, band, table, table,
            ],
            out_specs=[band, far, far, near, near],
            scratch_shapes=[
                pltpu.VMEM((2, prompt, HEAD_SIZE), BF16),
                pltpu.VMEM((2, prompt, HEAD_SIZE), BF16),
                pltpu.VMEM((pair, prompt), BF16),
            ],
        ),
        compiler_params=params(dimension_semantics=("arbitrary", "arbitrary")),
        name="attention_backward",
    )(flag, q_t, k, v, pk, pv, lse, up, mixed, cosine, sine)


def project_kernel(x_ref, gain_ref, w_ref, cos_ref, sin_ref, normed_ref, q_ref, k_ref, v_ref):
    x = x_ref[...].astype(F32)
    inverse = lax.rsqrt(jnp.mean(x * x, axis=-1, keepdims=True) + EPSILON)
    normed = (x * inverse * gain_ref[...].astype(F32)).astype(BF16)
    normed_ref[...] = normed
    members = w_ref.shape[0]
    kw = k_ref.shape[1] // members
    keys, values, queries = [], [], []
    for member in range(members):
        piece = dot_nn(normed, w_ref[member]).T
        keys.append(piece[:kw])
        values.append(piece[kw : 2 * kw])
        queries.append(piece[2 * kw :])
    cosine, sine = cos_ref[...], sin_ref[...]
    q_ref[...] = turn(jnp.concatenate(queries, axis=0), cosine, sine, 1.0).astype(BF16)
    k_ref[...] = turn(jnp.concatenate(keys, axis=0), cosine, sine, 1.0).T.astype(BF16)
    v_ref[...] = jnp.concatenate(values, axis=0).T.astype(BF16)


def project(x, gain, w, cosine, sine):
    rows, width = x.shape
    members = w.shape[0]
    qw = QUERY_HEADS * HEAD_SIZE
    kw = KEY_VALUE_HEADS * HEAD_SIZE
    band = pl.BlockSpec((ROWS, width), lambda i: (i, 0))
    table = pl.BlockSpec((HEAD_SIZE // 2, ROWS), lambda i: (0, i))
    thin = pl.BlockSpec((ROWS, kw), lambda i: (i, 0))
    return pl.pallas_call(
        project_kernel,
        out_shape=(
            jax.ShapeDtypeStruct((rows, width), BF16),
            jax.ShapeDtypeStruct((qw, rows), BF16),
            jax.ShapeDtypeStruct((rows, kw), BF16),
            jax.ShapeDtypeStruct((rows, kw), BF16),
        ),
        grid=(rows // ROWS,),
        in_specs=[
            band,
            pl.BlockSpec((1, width), lambda i: (0, 0)),
            pl.BlockSpec(w.shape, lambda i: (0, 0, 0), pipeline_mode=pl.Buffered(1)),
            table,
            table,
        ],
        out_specs=[band, pl.BlockSpec((qw, ROWS), lambda i: (0, i)), thin, thin],
        compiler_params=params(dimension_semantics=("arbitrary",)),
        name="project",
    )(x, gain, w, cosine, sine)


def finish_kernel(
    flag_ref, x_ref, gain_ref, w_ref, cos_ref, sin_ref, mid_ref, qraw_ref, far_ref, nk_ref, nv_ref,
    tokens_ref, gain_grad_ref, raw_ref,
):
    kw = nk_ref.shape[1]
    members = w_ref.shape[0]
    prompt = flag_ref[0] == 1
    far = far_ref[...].astype(F32)
    key_sum = jnp.where(prompt, far[:, :kw], nk_ref[...])
    value_raw = jnp.where(prompt, far[:, kw:], nv_ref[...]).astype(BF16)
    key_raw = turn(key_sum.T, cos_ref[...], sin_ref[...], -1.0).T.astype(BF16)
    query_raw = qraw_ref[...]
    ks = kw // members
    qs = query_raw.shape[1] // members
    normed_grad = None
    for member in range(members):
        raw = jnp.concatenate(
            [
                key_raw[:, member * ks : (member + 1) * ks],
                value_raw[:, member * ks : (member + 1) * ks],
                query_raw[:, member * qs : (member + 1) * qs],
            ],
            axis=1,
        )
        raw_ref[member] = raw
        part = dot_nt(raw, w_ref[member])
        normed_grad = part if normed_grad is None else normed_grad + part
    x = x_ref[...].astype(F32)
    width = x.shape[1]
    inverse = lax.rsqrt(jnp.mean(x * x, axis=-1, keepdims=True) + EPSILON)
    scaled = normed_grad * gain_ref[...].astype(F32)
    inner = jnp.sum(scaled * x, axis=-1, keepdims=True)
    rows_grad = scaled * inverse - x * (inverse**3 * inner / width)
    tokens_ref[...] = (mid_ref[...] + rows_grad).astype(BF16)

    @pl.when(pl.program_id(0) == 0)
    def _():
        gain_grad_ref[...] = jnp.zeros_like(gain_grad_ref)

    gain_grad_ref[...] += jnp.sum(normed_grad * x * inverse, axis=0, keepdims=True)


def finish(flag, x, gain, w, cosine, sine, middle_grad, query_raw, far, near_k, near_v):
    rows, width = x.shape
    kw = near_k.shape[1]
    band = pl.BlockSpec((ROWS, width), lambda i, f: (i, 0))
    row = pl.BlockSpec((1, width), lambda i, f: (0, 0))
    table = pl.BlockSpec((HEAD_SIZE // 2, ROWS), lambda i, f: (0, i))
    thin = pl.BlockSpec((ROWS, kw), lambda i, f: (i, 0))
    return pl.pallas_call(
        finish_kernel,
        out_shape=(
            jax.ShapeDtypeStruct((rows, width), BF16),
            jax.ShapeDtypeStruct((1, width), F32),
            jax.ShapeDtypeStruct((w.shape[0], rows, w.shape[2]), BF16),
        ),
        grid_spec=pltpu.PrefetchScalarGridSpec(
            num_scalar_prefetch=1,
            grid=(rows // ROWS,),
            in_specs=[
                band,
                row,
                pl.BlockSpec(w.shape, lambda i, f: (0, 0, 0), pipeline_mode=pl.Buffered(1)),
                table,
                table,
                band,
                pl.BlockSpec((ROWS, query_raw.shape[1]), lambda i, f: (i, 0)),
                pl.BlockSpec((ROWS, 2 * kw), lambda i, f: (i, 0)),
                thin,
                thin,
            ],
            out_specs=[
                band,
                row,
                pl.BlockSpec((w.shape[0], ROWS, w.shape[2]), lambda i, f: (0, i, 0)),
            ],
        ),
        compiler_params=params(dimension_semantics=("arbitrary",)),
        name="finish",
    )(flag, x, gain, w, cosine, sine, middle_grad, query_raw, far, near_k, near_v)


def spread_down(value, axis):
    size = lax.axis_size(axis)
    index = lax.axis_index(axis)
    bit = size // 2
    while bit >= 1:
        pairs = [(i, i + bit) for i in range(0, size, 2 * bit)]
        received = lax.ppermute(value, axis, pairs)
        value = jnp.where(index % (2 * bit) == bit, received, value)
        bit //= 2
    return value


def sum_up(value, axis):
    size = lax.axis_size(axis)
    bit = 1
    while bit < size:
        pairs = [(i + bit, i) for i in range(0, size, 2 * bit)]
        received = lax.ppermute(value, axis, pairs)
        value = (value.astype(F32) + received.astype(F32)).astype(value.dtype)
        bit *= 2
    return value


def assemble(piece, groups, members):
    height, width = piece.shape[1:]
    return (
        piece.reshape(groups, members, height, width)
        .transpose(0, 2, 1, 3)
        .reshape(groups * height, members * width)
    )


def disperse(full, groups, members):
    height = full.shape[0] // groups
    width = full.shape[1] // members
    return (
        full.reshape(groups, height, members, width)
        .transpose(0, 2, 1, 3)
        .reshape(groups * members, height, width)
    )


def gather(shard):
    return lax.all_gather(shard[None], ("grp", "mem"), axis=0, tiled=True)


def scatter(terms):
    return lax.psum_scatter(terms, ("grp", "mem"), scatter_dimension=0, tiled=True)[0].astype(F32)


def body(
    tokens, attn_gain, mlp_gain, query_weight, key_matrix, value_matrix, output_weight,
    gate_weight, up_weight, down_weight, cotangent,
):
    groups = lax.axis_size("grp")
    members = lax.axis_size("mem")
    qs = query_weight.shape[1]
    ks = key_matrix.shape[1]
    fs = gate_weight.shape[1]
    height = query_weight.shape[0]
    narrow = 2 * ks + qs
    gains = jnp.pad(jnp.stack([attn_gain, mlp_gain]), ((0, 6), (0, narrow - attn_gain.shape[0])))
    first = jnp.concatenate(
        [jnp.concatenate([key_matrix, value_matrix, query_weight], axis=1), gains], axis=0
    )
    first = gather(first)
    second = gather(output_weight)
    third = gather(jnp.concatenate([gate_weight, up_weight], axis=1))
    fourth = gather(down_weight)
    gain_rows = first[:members, height : height + 2, : attn_gain.shape[0]]
    gain_one = gain_rows[:, 0].reshape(1, -1)
    gain_two = gain_rows[:, 1].reshape(1, -1)
    w_qkv = (
        first[:, :height]
        .reshape(groups, members, height, narrow)
        .transpose(1, 0, 2, 3)
        .reshape(members, groups * height, narrow)
    )
    prompt_flag = lax.axis_index("mem") == 0
    flag = prompt_flag.astype(jnp.int32).reshape(1)
    x = tokens[0]
    rows = x.shape[0]
    local = jnp.arange(rows)
    positions = jnp.where(prompt_flag, local, rows + local % CONT_LEN).astype(F32)
    half = HEAD_SIZE // 2
    freq = 10000.0 ** (-jnp.arange(half, dtype=F32) * 2.0 / HEAD_SIZE)
    angle = freq[:, None] * positions[None, :]
    cosine, sine = jnp.cos(angle), jnp.sin(angle)
    normed, q_t, k, v = project(x, gain_one, w_qkv, cosine, sine)
    kw = k.shape[1]
    common = spread_down(jnp.concatenate([k, v], axis=1), "mem")
    pk, pv = common[:, :kw], common[:, kw:]
    mixed, lse = attention_forward(flag, q_t, k, v, pk, pv)
    w_out = assemble(second, groups, members)
    w_gate = assemble(third[:, :, :fs], groups, members)
    w_up = assemble(third[:, :, fs:], groups, members)
    w_down = assemble(fourth, groups, members)
    middle = x.astype(F32) + dot_nn(mixed, w_out)
    inverse_two = lax.rsqrt(jnp.mean(middle * middle, axis=-1, keepdims=True) + EPSILON)
    gain_two = gain_two.astype(F32)
    normed_two = (middle * inverse_two * gain_two).astype(BF16)
    gate = dot_nn(normed_two, w_gate)
    up = dot_nn(normed_two, w_up)
    sigma = jax.nn.sigmoid(gate)
    hidden = (gate * sigma * up).astype(BF16)
    output = (middle + dot_nn(hidden, w_down)).astype(BF16)[None]
    upstream = cotangent[0]
    down_grad = scatter(disperse(dot_tn(hidden, upstream).astype(BF16), groups, members))
    hidden_grad = dot_nt(upstream, w_down)
    gate_grad = (hidden_grad * up * sigma * (1.0 + gate * (1.0 - sigma))).astype(BF16)
    up_grad = (hidden_grad * gate * sigma).astype(BF16)
    pair_grad = scatter(
        jnp.concatenate(
            [
                disperse(dot_tn(normed_two, gate_grad).astype(BF16), groups, members),
                disperse(dot_tn(normed_two, up_grad).astype(BF16), groups, members),
            ],
            axis=2,
        )
    )
    normed_two_grad = dot_nt(gate_grad, w_gate) + dot_nt(up_grad, w_up)
    scaled = normed_two_grad * gain_two
    mlp_gain_grad = jnp.sum(normed_two_grad * middle * inverse_two, axis=0)
    inner = jnp.sum(scaled * middle, axis=-1, keepdims=True)
    middle_grad = (
        upstream.astype(F32)
        + scaled * inverse_two
        - middle * (inverse_two**3 * inner / middle.shape[-1])
    )
    middle_low = middle_grad.astype(BF16)
    mixed_grad = dot_nt(middle_low, w_out).astype(BF16)
    query_raw, far_k, far_v, near_k, near_v = attention_backward(
        flag, q_t, k, v, pk, pv, lse, mixed_grad, mixed, cosine, sine
    )
    far = sum_up(jnp.concatenate([far_k, far_v], axis=1).astype(BF16), "mem")
    tokens_grad, attn_gain_grad, raw = finish(
        flag, x, gain_one, w_qkv, cosine, sine, middle_grad, query_raw, far, near_k, near_v
    )
    out_terms = disperse(dot_tn(mixed, middle_low).astype(BF16), groups, members)
    qkv_terms = jnp.stack(
        [
            dot_tn(normed, raw[member]).astype(BF16).reshape(groups, height, narrow)
            for member in range(members)
        ],
        axis=1,
    ).reshape(groups * members, height, narrow)
    gain_terms = jnp.stack([attn_gain_grad[0], mlp_gain_grad]).astype(BF16)
    gain_terms = gain_terms.reshape(2, members, -1).transpose(1, 0, 2)
    gain_terms = jnp.pad(
        jnp.tile(gain_terms, (groups, 1, 1)), ((0, 0), (0, 6), (0, narrow - gain_terms.shape[2]))
    )
    last = scatter(
        jnp.concatenate(
            [
                jnp.concatenate([qkv_terms, gain_terms], axis=1),
                jnp.pad(out_terms, ((0, 0), (0, 8), (0, 0))),
            ],
            axis=2,
        )
    )
    gs = attn_gain.shape[0]
    return (
        output,
        tokens_grad[None],
        last[height, :gs],
        last[height + 1, :gs],
        last[:height, 2 * ks : narrow],
        last[:height, :ks],
        last[:height, ks : 2 * ks],
        last[:height, narrow:],
        pair_grad[:, :fs],
        pair_grad[:, fs:],
        down_grad,
    )


def solution(mesh):
    rows = P("grp", "mem", None)
    both = P("grp", "mem")
    gain = P("mem")
    return jax.shard_map(
        body,
        mesh=mesh,
        in_specs=(rows, gain, gain) + (both,) * 7 + (rows,),
        out_specs=(rows, rows, gain, gain) + (both,) * 7,
        check_vma=False,
    )
```

time: 1960 us -> 941 us (0.48)
  waiting for transfers between devices: 1110 us -> 399 us
  matrix products: 371 us -> 161 us
  Pallas kernels: 0 us -> 141 us
  blocking collectives: 128 us -> 0 us
  other arithmetic: 99.3 us -> 39.4 us
  local copies, waits for them, and re-layouts: 213 us -> 169 us
    reduce_scatter x7 -> x3, waiting for transfers between devices: 913 us -> 195 us  [scatter(): lax.psum_scatter(terms, ('grp', 'mem'), scatter_dimension=0, tiled=True)[0]]
    dot_general x35 -> x16, matrix products: 371 us -> 161 us  [the longest x8 61.5 us: dot_tn(): lax.dot_general(left, right, (((0,), (0,)), ((), ())), preferred_element_...]
    psum x2 -> x0, waiting for transfers between devices: 151 us -> none  [the longest x1 142 us: body(): lax.psum(distant_key.reshape(row_count, KEY_VALUE_HEADS * HEAD_SIZE).asty...]
    pallas_call x0 -> x4, Pallas kernels: none -> 141 us  [the longest x1 59.7 us: attention_backward(): pl.pallas_call(backward_kernel, out_shape=(jax.ShapeDtypeStruct((rows, q_...]
    all_gather x5 -> x4, waiting for transfers between devices: 39 us -> 154 us  [gather(): return lax.all_gather(shard[None], ('grp', 'mem'), axis=0, tiled=True)]
    all_gather x2 -> x0, blocking collectives: 89.3 us -> none  [the longest x1 48.2 us: body(): lax.all_gather(shards[3], ('grp', 'mem'), axis=0, tiled=True)]
    ppermute x0 -> x4, waiting for transfers between devices: none -> 48.8 us  [the longest x2 26.4 us: sum_up(): received = lax.ppermute(value, axis, pairs)]
    unnamed x1 -> x0, blocking collectives: 38.4 us -> none
  transfers between devices with their start and end apart: 15 -> 11, of which waited for: 10 -> 9; matrix products, arithmetic and copies ran while one was open for 19% -> 23% of each run, Pallas kernels for 0% -> 15%
where the time goes in v1:
time: 941 us; the launch traced here: 934 us
  waiting for transfers between devices  399 us (42%)
  local copies, waits for them, and re-layouts  169 us (18%)
  matrix products  161 us (17%)
  Pallas kernels  141 us (15%)
  other arithmetic  39.4 us (4%)
  between operations  14.7 us (2%)
    reduce_scatter x3, waiting for transfers between devices, scatter(): lax.psum_scatter(terms, ('grp', 'mem'), scatter_dimension=0, tiled=True)[0]  195 us
    all_gather x4, waiting for transfers between devices, gather(): return lax.all_gather(shard[None], ('grp', 'mem'), axis=0, tiled=True)  154 us
    dot_general x8, matrix products, dot_tn(): lax.dot_general(left, right, (((0,), (0,)), ((), ())), preferred_element_...  61.5 us
    pallas_call x1, Pallas kernels, attention_backward(): pl.pallas_call(backward_kernel, out_shape=(jax.ShapeDtypeStruct((rows, q_...  59.7 us
    dot_general x4, matrix products, dot_nt(): lax.dot_general(left, right, (((1,), (1,)), ((), ())), preferred_element_...  56.4 us
    pallas_call x1, Pallas kernels, attention_forward(): pl.pallas_call(forward_kernel, out_shape=(jax.ShapeDtypeStruct((rows, q_t...  56.2 us
    dot_general x4, matrix products, dot_nn(): lax.dot_general(left, right, (((1,), (0,)), ((), ())), preferred_element_...  43.4 us
    reshape x3, local copies, waits for them, and re-layouts, disperse(): full.reshape(groups, height, members, width).transpose(0, 2, 1, 3)  32.6 us
  transfers between devices with their start and end apart: 11, of which 9 were waited for; matrix products, arithmetic and copies ran while one was open for 23% of the time, Pallas kernels for 15%

profile of v1, /device:TPU:0, one launch (start us, length us, event | category | flops | bytes accessed | tf_op | source)
XLA Modules:
  0.0 934.2 jit_solution(1729715071264465159)
XLA Ops:
  8.6 1.7 pad_maximum_fusion.4
  11.9 1.8 pad_maximum_fusion.3
  15.1 63.7 %all-gather.9.cloned.1.call-done = bf16[4864,480]{1,0:T(8,128)(2,1)} async-done(((bf16[152,480]{1,0:T(8,128)(2,1)}), bf16[4864,480]{1,0:T(8,128)(2,1)}) %all-gather.9.cloned.1.call-update) | async-done | bytes 4669456 | tf_op jit(solution)/shard_map/all_gather | solution.py:446
  78.7 4.9 slice.80
  85.1 4.9 copy.41
  89.9 11.1 %project.1 = (bf16[1024,1152]{1,0:T(8,128)(2,1)}, bf16[1152,1024]{1,0:T(8,128)(2,1)}, bf16[1024,384]{1,0:T(8,128)(2,1)}, bf16[1024,384]{1,0:T(8,128)(2,1)}) custom-call(bf16[1024,1152]{1,0:T(8,128)(2,1)} %bitcast.133, bf16[1,1152]{1,0:T(2,128)(2,1)} %reshape_squeeze.4.gain_ref, bf16[4,1152,480]{2,1,0:T(8,128)(2,1)} %bitcast.111, ...), custom_call_target="tpu_custom_call" | custom-call | tf_op jit(solution)/shard_map/project/pallas_call | solution.py:299
  103.6 3.5 collective-permute-start
  107.1 22.3 %collective-permute-done = bf16[1024,768]{1,0:T(8,128)(2,1)S(1)} collective-permute-done((bf16[1024,768]{1,0:T(8,128)(2,1)S(1)}, bf16[1024,768]{1,0:T(8,128)(2,1)S(1)}, u32[]{:S(2)}, u32[]{:S(2)}) %collective-permute-start) | collective-permute-done | bytes 1572896 | tf_op jit(solution)/shard_map/ppermute | solution.py:409
  130.7 2.5 collective-permute-start.1
  133.2 6.8 all-gather.11.cloned.1.call-done
  140.0 3.5 copy.62
  143.5 3.7 reshape.153
  150.9 56.2 %attention_forward.1 = (bf16[1024,1152]{1,0:T(8,128)(2,1)}, f32[3,8,1024]{2,1,0:T(8,128)}) custom-call(s32[1]{0:T(128)} %bitcast.1.flag_ref, bf16[1152,1024]{1,0:T(8,128)(2,1)} %get-tuple-element.25.q_ref, bf16[1024,384]{1,0:T(8,128)(2,1)} %get-tuple-element.26.k_ref, bf16[1024,384]{1,0:T(8,128)(2,1)} %get-tuple-element.27.v_ref, ...), custom_call_target="tpu_custom_call" | custom-call | tf_op jit(solution)/shard_map/attention_forward/pallas_call | solution.py:116
  207.1 5.4 multiply_reduce_fusion.2
  212.5 2.1 copy-done
  215.5 12.2 %reshape.158 = bf16[8,4,384,288]{2,1,0,3:T(4,128)(2,1)} reshape(bf16[12288,288]{0,1:T(8,128)(2,1)} %all-gather.15.cloned.1.call-done) | data formatting | bytes 14155776 | tf_op jit(solution)/shard_map/reshape | solution.py:429
  227.7 3.9 copy.45
  231.6 4.7 copy.59
  236.3 83.3 %all-gather.13.cloned.1.call-done = bf16[4608,1536]{1,0:T(8,128)(2,1)} async-done(((bf16[144,1536]{1,0:T(8,128)(2,1)}), bf16[4608,1536]{1,0:T(8,128)(2,1)}) %all-gather.13.cloned.1.call-update) | async-done | bytes 14155792 | tf_op jit(solution)/shard_map/all_gather | solution.py:446
  319.6 10.1 %fusion.35 = (bf16[32,144,768]{2,1,0:T(8,128)(2,1)}, bf16[32,144,768]{2,1,0:T(8,128)(2,1)}) fusion(bf16[32,144,1536]{2,1,0:T(8,128)(2,1)} %bitcast.129), kind=kLoop, calls=%fused_computation.89 | loop fusion | bytes 28311552 | tf_op jit(solution)/shard_map/slice | solution.py:497
  329.7 9.5 %copy.43 = bf16[8,144,4,768]{3,2,1,0:T(4,128)(2,1)} copy(bf16[8,144,4,768]{3,1,2,0:T(8,128)(2,1)} %bitcast.117) | data formatting | bytes 14155776 | tf_op jit(solution)/shard_map/transpose | solution.py:430
  339.2 7.5 copy.57
  346.8 9.5 %copy.44 = bf16[8,144,4,768]{3,2,1,0:T(4,128)(2,1)} copy(bf16[8,144,4,768]{3,1,2,0:T(8,128)(2,1)} %bitcast.116) | data formatting | bytes 14155776 | tf_op jit(solution)/shard_map/transpose | solution.py:430
  356.3 4.8 copy.58
  361.1 10.9 %fusion.41 = f32[1024,3072]{1,0:T(8,128)} fusion(bf16[1024,1152]{1,0:T(8,128)(2,1)S(1)} %multiply_convert_fusion.3, bf16[1152,3072]{1,0:T(8,128)(2,1)S(1)} %bitcast.141), kind=kOutput, calls=%fused_computation.95 | convolution fusion | flops 7247757312 | bytes 22020096 | tf_op jit(solution)/shard_map/dot_general | solution.py:24
  372.0 12.5 %fusion.40 = f32[1024,3072]{1,0:T(8,128)} fusion(bf16[1024,1152]{1,0:T(8,128)(2,1)} %copy-done.8, bf16[1152,3072]{1,0:T(8,128)(2,1)S(1)} %bitcast.140), kind=kOutput, calls=%fused_computation.94 | convolution fusion | flops 7247757312 | bytes 22020096 | tf_op jit(solution)/shard_map/dot_general | solution.py:24
  384.6 23.2 %multiply_convert_fusion = (bf16[1024,3072]{1,0:T(8,128)(2,1)}, bf16[1024,3072]{1,0:T(8,128)(2,1)}, bf16[1024,3072]{1,0:T(8,128)(2,1)}) fusion(f32[1024,3072]{1,0:T(8,128)} %fusion.40, f32[1024,3072]{1,0:T(8,128)} %fusion.41, bf16[3072,1152]{0,1:T(8,128)(2,1)} %bitcast.135, bf16[1,1024,1152]{2,1,0:T(8,128)(2,1)S(1)} %copy-done.7), kind=kOutput, calls=%fused_computation.8 | convolution fusion | flops 7298088960 | bytes 53477376 | tf_op jit(solution)/shard_map/dot_general | solution.py:28
  407.8 14.0 %fusion.42 = f32[1024,1152]{1,0:T(8,128)} fusion(bf16[1024,3072]{1,0:T(8,128)(2,1)} %get-tuple-element.44, bf16[1152,3072]{1,0:T(8,128)(2,1)} %bitcast.137), kind=kOutput, calls=%fused_computation.96 | convolution fusion | flops 7247757312 | bytes 18087936 | tf_op jit(solution)/shard_map/dot_general | solution.py:28
  421.8 14.3 %multiply_reduce_fusion = (bf16[1152]{0:T(1024)(128)(2,1)S(1)}, f32[1024]{0:T(1024)S(1)}, f32[1024,1152]{1,0:T(8,128)}) fusion(f32[1024,1152]{1,0:T(8,128)} %copy-done, f32[1024]{0:T(1024)S(1)} %add_rsqrt_fusion, f32[1152]{0:T(1024)S(1)} %reshape.171, f32[1024,1152]{1,0:T(8,128)} %fusion.42, bf16[1024,3072]{1,0:T(8,128)(2,1)} %get-tuple-element.43, ...), kind=kOutput, calls=%fused_computation.19 | convolution fusion | flops 7256012800 | bytes 27540224 | tf_op jit(solution)/shard_map/dot_general | solution.py:28
  436.1 12.3 %convolution_convert_fusion = bf16[3072,1152]{1,0:T(8,128)(2,1)} fusion(bf16[1024,3072]{1,0:T(8,128)(2,1)} %get-tuple-element.45, bf16[1,1024,1152]{2,1,0:T(8,128)(2,1)S(1)} %copy-done.7), kind=kOutput, calls=%fused_computation.12 | convolution fusion | flops 7251296256 | bytes 15728640 | tf_op jit(solution)/shard_map/dot_general | solution.py:32
  448.4 10.3 %copy.55 = bf16[3072,1152]{0,1:T(8,128)(2,1)} copy(bf16[3072,1152]{1,0:T(8,128)(2,1)} %convolution_convert_fusion) | data formatting | bytes 14155776 | tf_op jit(solution)/shard_map/convert_element_type | solution.py:510
  458.7 4.7 copy.60
  463.4 4.0 copy.56
  467.5 4.8 multiply_subtract_fusion.mid_ref
  472.3 4.8 convolution_convert_fusion.4.up_ref
  477.1 59.7 %attention_backward.1 = (bf16[1024,1152]{1,0:T(8,128)(2,1)}, f32[1024,384]{1,0:T(8,128)}, f32[1024,384]{1,0:T(8,128)}, f32[1024,384]{1,0:T(8,128)}, f32[1024,384]{1,0:T(8,128)}) custom-call(s32[1]{0:T(128)} %bitcast.1.flag_ref, bf16[1152,1024]{1,0:T(8,128)(2,1)} %get-tuple-element.25.q_ref, bf16[1024,384]{1,0:T(8,128)(2,1)} %get-tuple-element.26.k_ref, ...), custom_call_target="tpu_custom_call" | custom-call | tf_op jit(solution)/shard_map/attention_backward/pallas_call | solution.py:242
  541.3 17.2 %collective-permute-done.2 = bf16[1024,768]{1,0:T(8,128)(2,1)S(1)} collective-permute-done((bf16[1024,768]{1,0:T(8,128)(2,1)S(1)}, bf16[1024,768]{1,0:T(8,128)(2,1)S(1)}, u32[]{:S(2)}, u32[]{:S(2)}) %collective-permute-start.2) | collective-permute-done | bytes 1572896 | tf_op jit(solution)/shard_map/ppermute | solution.py:420
  561.4 6.4 convolution_convert_fusion.3
  567.8 4.6 reshape.161
  572.4 2.5 copy.52
  574.9 9.3 collective-permute-done.3
  584.2 3.5 add_convert_fusion.1.far_ref
  587.7 14.3 %finish.1 = (bf16[1024,1152]{1,0:T(8,128)(2,1)}, f32[1,1152]{1,0:T(1,128)}, bf16[4,1024,480]{2,1,0:T(8,128)(2,1)}) custom-call(s32[1]{0:T(128)} %bitcast.1.flag_ref, bf16[1024,1152]{1,0:T(8,128)(2,1)} %bitcast.134, bf16[1,1152]{1,0:T(2,128)(2,1)} %reshape_squeeze.4.gain_ref, bf16[4,1152,480]{2,1,0:T(8,128)(2,1)} %bitcast.112, ...), custom_call_target="tpu_custom_call" | custom-call | tf_op jit(solution)/shard_map/finish/pallas_call | solution.py:370
  602.9 4.4 convolution_convert_fusion.5
  607.3 2.4 copy.49
  609.7 4.4 convolution_convert_fusion.6
  614.1 2.4 copy.48
  616.5 4.5 convolution_convert_fusion.8
  621.0 2.4 copy.46
  623.4 4.5 convolution_convert_fusion.7
  627.9 2.4 copy.47
  630.3 2.7 pad_maximum_fusion.1
  633.5 4.3 fusion.4
  639.4 12.6 %convolution_convert_fusion.2 = bf16[1152,3072]{1,0:T(8,128)(2,1)} fusion(bf16[1024,1152]{1,0:T(8,128)(2,1)S(1)} %copy-done.9, bf16[1024,3072]{1,0:T(8,128)(2,1)} %get-tuple-element.44), kind=kOutput, calls=%fused_computation.14 | convolution fusion | flops 7251296256 | bytes 15728640 | tf_op jit(solution)/shard_map/dot_general | solution.py:32
  652.0 14.0 %reshape.163 = bf16[8,144,4,768]{3,2,1,0:T(4,128)(2,1)} reshape(bf16[1152,3072]{1,0:T(8,128)(2,1)} %convolution_convert_fusion.2) | data formatting | bytes 14155776 | tf_op jit(solution)/shard_map/reshape | solution.py:439
  666.0 7.2 copy.53
  673.2 12.5 %convolution_convert_fusion.1 = bf16[1152,3072]{1,0:T(8,128)(2,1)} fusion(bf16[1024,1152]{1,0:T(8,128)(2,1)S(1)} %copy-done.9, bf16[1024,3072]{1,0:T(8,128)(2,1)} %get-tuple-element.43), kind=kOutput, calls=%fused_computation.13 | convolution fusion | flops 7251296256 | bytes 15728640 | tf_op jit(solution)/shard_map/dot_general | solution.py:32
  685.7 14.0 %reshape.165 = bf16[8,144,4,768]{3,2,1,0:T(4,128)(2,1)} reshape(bf16[1152,3072]{1,0:T(8,128)(2,1)} %convolution_convert_fusion.1) | data formatting | bytes 14155776 | tf_op jit(solution)/shard_map/reshape | solution.py:439
  699.7 4.3 copy.54
  704.8 5.9 pad_maximum_fusion
  710.7 14.5 %fusion.6 = bf16[1,1024,1152]{2,1,0:T(8,128)(2,1)} fusion(f32[1024,1152]{1,0:T(8,128)} %copy-done, bf16[1024,3072]{1,0:T(8,128)(2,1)} %get-tuple-element.45, bf16[3072,1152]{0,1:T(8,128)(2,1)} %bitcast.136), kind=kOutput, calls=%fused_computation.29 | convolution fusion | flops 7250116608 | bytes 20447232 | tf_op jit(solution)/shard_map/dot_general | solution.py:24
  725.3 1.7 bitcast_convert_fusion.2
  727.0 30.6 %reduce-scatter.4.cloned.1.call-done = bf16[1,152,768]{2,1,0:T(8,128)(2,1)} async-done(((bf16[32,152,768]{2,1,0:T(8,128)(2,1)}), bf16[1,152,768]{2,1,0:T(8,128)(2,1)}) %reduce-scatter.4.cloned.1.call-update) | async-done | bytes 233488 | tf_op jit(solution)/shard_map/reduce_scatter | solution.py:450
  760.9 164.2 %reduce-scatter.6.cloned.1.call-done = bf16[1,144,1536]{2,1,0:T(8,128)(2,1)} async-done(((bf16[32,144,1536]{2,1,0:T(8,128)(2,1)}), bf16[1,144,1536]{2,1,0:T(8,128)(2,1)}) %reduce-scatter.6.cloned.1.call-update) | async-done | bytes 442384 | tf_op jit(solution)/shard_map/reduce_scatter | solution.py:450
  (83 shorter events, 30.7 us)
Async XLA Ops:
  7.2 71.6 %all-gather.9.cloned.1.call-start = ((), (), s32[]{:S(2)}) async-start(), calls=%async_computation.6 | async-start | bytes 5136384 | tf_op jit(solution)/shard_map/all_gather | solution.py:446
  10.3 129.6 %all-gather.11.cloned.1.call-start = ((), (), s32[]{:S(2)}) async-start(), calls=%async_computation.7 | async-start | bytes 3649536 | tf_op jit(solution)/shard_map/all_gather | solution.py:446
  11.1 204.5 %all-gather.15.cloned.1.call-start = ((), (), s32[]{:S(2)}) async-start(), calls=%async_computation.9 | async-start | bytes 7299072 | tf_op jit(solution)/shard_map/all_gather | solution.py:446
  11.8 307.8 %all-gather.13.cloned.1.call-start = ((), (), s32[]{:S(2)}) async-start(), calls=%async_computation.8 | async-start | bytes 14598144 | tf_op jit(solution)/shard_map/all_gather | solution.py:446
  13.7 711.5 %reduce-scatter.8.cloned.1.call-start = ((), (), s32[]{:S(2)}) async-start(), calls=%async_computation.5 | async-start | bytes 7299072 | tf_op jit(solution)/shard_map/reduce_scatter | solution.py:450
  103.6 25.8 %collective-permute-start = (bf16[1024,768]{1,0:T(8,128)(2,1)S(1)}, bf16[1024,768]{1,0:T(8,128)(2,1)S(1)}, u32[]{:S(2)}, u32[]{:S(2)}) collective-permute-start(bf16[1024,768]{1,0:T(8,128)(2,1)S(1)} %constant_dynamic-update-slice_fusion), channel_id=1, source_target_pairs={{0,2},{4,6},{8,10},{12,14},{16,18},{20,22},{24,26},{28,30}} | collective-permute-start | bytes 4718600 | tf_op jit(solution)/shard_map/ppermute | solution.py:409
  130.7 17.3 %collective-permute-start.1 = (bf16[1024,768]{1,0:T(8,128)(2,1)}, bf16[1024,768]{1,0:T(8,128)(2,1)}, u32[]{:S(2)}, u32[]{:S(2)}) collective-permute-start(bf16[1024,768]{1,0:T(8,128)(2,1)} %broadcast_select_fusion), channel_id=1, source_target_pairs={{0,1},{2,3},{4,5},{6,7},{8,9},{10,11},{12,13},{14,15},{16,17},{18,... | collective-permute-start | bytes 4718600 | tf_op jit(solution)/shard_map/ppermute | solution.py:409
  149.6 57.6 %copy-start.2 = (bf16[1,1024,1152]{2,1,0:T(8,128)(2,1)S(1)}, bf16[1,1024,1152]{2,1,0:T(8,128)(2,1)}, u32[]{:S(2)}) copy-start(bf16[1,1024,1152]{2,1,0:T(8,128)(2,1)} %param.11) | copy-start | bytes 7077892
  149.6 57.5 %copy-start.5 = (bf16[1152,1152]{1,0:T(8,128)(2,1)S(1)}, bf16[1152,1152]{1,0:T(8,128)(2,1)}, u32[]{:S(2)}) copy-start(bf16[1152,1152]{1,0:T(8,128)(2,1)} %reshape.153) | copy-start | bytes 7962628
  212.5 2.1 copy-start
  215.1 145.9 %copy-start.8 = (bf16[1024,1152]{1,0:T(8,128)(2,1)}, bf16[1024,1152]{1,0:T(8,128)(2,1)S(1)}, u32[]{:S(2)}) copy-start(bf16[1024,1152]{1,0:T(8,128)(2,1)S(1)} %multiply_convert_fusion.3) | copy-start | bytes 7077892
  356.3 15.8 %slice-start.2 = ((s8[7077888]{0:T(1024)(128)(4,1)}), s8[2883584]{0:T(1024)(128)(4,1)S(1)}, s32[]{:S(2)}) async-start(s8[7077888]{0:T(1024)(128)(4,1)} %bitcast.138), calls=%async_computation.12 | async-start | bytes 5767168
  361.1 10.9 %copy-start.3 = (bf16[144,8,4,768]{3,1,2,0:T(8,128)(2,1)}, bf16[144,8,4,768]{3,1,2,0:T(8,128)(2,1)S(1)}, u32[]{:S(2)}) copy-start(bf16[144,8,4,768]{3,1,2,0:T(8,128)(2,1)S(1)} %copy.58) | copy-start | bytes 21233668
  361.1 10.9 %slice-start.3 = ((s8[7077888]{0:T(1024)(128)(4,1)}), s8[4194304]{0:T(1024)(128)(4,1)S(1)}, s32[]{:S(2)}) async-start(s8[7077888]{0:T(1024)(128)(4,1)} %bitcast.138), calls=%async_computation.13 | async-start | bytes 8388608
  372.0 12.5 %copy-start.7 = (bf16[1,1024,1152]{2,1,0:T(8,128)(2,1)S(1)}, bf16[1,1024,1152]{2,1,0:T(8,128)(2,1)}, u32[]{:S(2)}) copy-start(bf16[1,1024,1152]{2,1,0:T(8,128)(2,1)} %param.21) | copy-start | bytes 7077892
  407.8 14.1 %copy-start.4 = (bf16[144,8,4,768]{3,1,2,0:T(8,128)(2,1)S(1)}, bf16[144,8,4,768]{3,1,2,0:T(8,128)(2,1)}, u32[]{:S(2)}) copy-start(bf16[144,8,4,768]{3,1,2,0:T(8,128)(2,1)} %copy-done.3) | copy-start | bytes 21233668
  467.4 290.2 %reduce-scatter.4.cloned.1.call-start = ((), (), s32[]{:S(2)}) async-start(), calls=%async_computation.3 | async-start | bytes 7704576 | tf_op jit(solution)/shard_map/reduce_scatter | solution.py:450
  467.5 4.8 copy-start.6
  472.3 4.8 copy-start.1
  540.0 18.5 %collective-permute-start.2 = (bf16[1024,768]{1,0:T(8,128)(2,1)S(1)}, bf16[1024,768]{1,0:T(8,128)(2,1)S(1)}, u32[]{:S(2)}, u32[]{:S(2)}) collective-permute-start(bf16[1024,768]{1,0:T(8,128)(2,1)S(1)} %pad_maximum_fusion.2), channel_id=1, source_target_pairs={{1,0},{3,2},{5,4},{7,6},{9,8},{11,10},{13,12},{15,14},{17,16},{19,... | collective-permute-start | bytes 4718600 | tf_op jit(solution)/shard_map/ppermute | solution.py:420
  560.0 24.2 %collective-permute-start.3 = (bf16[1024,768]{1,0:T(8,128)(2,1)}, bf16[1024,768]{1,0:T(8,128)(2,1)}, u32[]{:S(2)}, u32[]{:S(2)}) collective-permute-start(bf16[1024,768]{1,0:T(8,128)(2,1)} %add_convert_fusion.2), channel_id=1, source_target_pairs={{2,0},{6,4},{10,8},{14,12},{18,16},{22,20},{26,24},{30,28}} | collective-permute-start | bytes 4718600 | tf_op jit(solution)/shard_map/ppermute | solution.py:420
  637.8 1.7 copy-start.9
  637.8 287.3 %reduce-scatter.6.cloned.1.call-start = ((), (), s32[]{:S(2)}) async-start(), calls=%async_computation.4 | async-start | bytes 14598144 | tf_op jit(solution)/shard_map/reduce_scatter | solution.py:450
  699.6 4.3 slice-start
  699.6 5.1 slice-start.1
Sparse Core Ops, SparseCore 0:
  11.4 67.2 all-gather.8
  81.7 58.2 all-gather.10
  142.9 72.6 all-gather.14
  218.9 100.6 all-gather.12
  467.5 117.8 reduce-scatter.7
  637.9 119.6 reduce-scatter.3
  763.6 161.4 reduce-scatter.5
